TPU v7x, 512 devices: a whole 4x4x16 slice. The times are simulated.
512 devices in a mesh: shard: 32 (over z, core), tensor: 4 (over x), section: 4 (over y).
Axes of the slice: x: 4, y: 4, z: 16, core: 2. Of those that a mesh axis runs over, the one named last changes fastest.
Arguments:
- proj_grads: bfloat16 [4, 32, 2, 2048, 1024], P('section', 'shard', None, None, 'tensor'), as said below
- beta_grads: bfloat16 [4, 32, 2, 16, 2048], P('section', 'shard', None, 'tensor'), as said below
- gain_grads: bfloat16 [4, 32, 4, 2, 2048], P('section', 'shard', 'tensor'), as said below
- proj_master: float32 [4, 2048, 1024], P('section', 'shard', 'tensor'), may hold values from -0.25 to 0.25
- proj_moment: float32 [4, 2048, 1024], P('section', 'shard', 'tensor'), may hold values from -0.6 to 0.6
- proj_second: float32 [4, 2048, 1024], P('section', 'shard', 'tensor'), may hold values from 0.01 to 1
- beta_master: float32 [4, 16, 2048], P('section', 'tensor', 'shard'), may hold values from -0.25 to 0.25
- beta_moment: float32 [4, 16, 2048], P('section', 'tensor', 'shard'), may hold values from -0.6 to 0.6
- beta_second: float32 [4, 16, 2048], P('section', 'tensor', 'shard'), may hold values from 0.01 to 1
- gain_master: float32 [4, 2048], P('section', ('shard', 'tensor')), may hold values from 0.4 to 0.75
- gain_moment: float32 [4, 2048], P('section', ('shard', 'tensor')), may hold values from -0.6 to 0.6
- gain_second: float32 [4, 2048], P('section', ('shard', 'tensor')), may hold values from 0.01 to 1
- learn_rate: float32 [], replicated, may hold values from 0.01 to 0.04
- clip_limit: float32 [], replicated, may hold values from 730.063 to 2336.2016
Outputs:
- proj_weights: bfloat16 [4, 2048, 1024], P('section', None, 'tensor')
- beta_weights: bfloat16 [4, 16, 2048], P('section', 'tensor')
- gain_weights: bfloat16 [4, 2048], P('section')
- proj_master_new: float32 [4, 2048, 1024], P('section', 'shard', 'tensor')
- proj_moment_new: float32 [4, 2048, 1024], P('section', 'shard', 'tensor')
- proj_second_new: float32 [4, 2048, 1024], P('section', 'shard', 'tensor')
- beta_master_new: float32 [4, 16, 2048], P('section', 'tensor', 'shard')
- beta_moment_new: float32 [4, 16, 2048], P('section', 'tensor', 'shard')
- beta_second_new: float32 [4, 16, 2048], P('section', 'tensor', 'shard')
- gain_master_new: float32 [4, 2048], P('section', ('shard', 'tensor'))
- gain_moment_new: float32 [4, 2048], P('section', ('shard', 'tensor'))
- gain_second_new: float32 [4, 2048], P('section', ('shard', 'tensor'))
- grad_rms: float32 [], replicated
Inputs may be any that keep to these rules, and one draw needn't show every extreme that they name: `proj_grads`: finite gradient values. `beta_grads`: finite gradient values. `gain_grads`: finite gradient values.
All inputs are finite; a program needn't handle non-finite values.
Results may differ from a plain program's by a relative error of at most 0.0005.
Values may be sent and summed in bfloat16 or wider, within the bound.
No kernel may reach another device: no remote copies, remote signals or barrier semaphores. Data moves between devices by JAX's collectives and lax.ppermute only.
A program may use at most 64 MiB of HBM per device.

v0:
```python
import jax
import jax.numpy as jnp
from jax import lax
from jax.sharding import PartitionSpec as P

first_beta = 0.9
second_beta = 0.95
decay_rate = 0.1
adam_eps = 1e-08
norm_eps = 1e-06


def adam_update(grad, factor, learn_rate, master, moment, second):
    clipped = grad * factor
    moment_new = first_beta * moment + (1.0 - first_beta) * clipped
    second_new = second_beta * second + (1.0 - second_beta) * clipped * clipped
    master_new = master * (1.0 - learn_rate * decay_rate) - learn_rate * moment_new / (
        jnp.sqrt(second_new) + adam_eps
    )
    return (master_new, moment_new, second_new)


def per_device(
    proj_grads,
    beta_grads,
    gain_grads,
    proj_master,
    proj_moment,
    proj_second,
    beta_master,
    beta_moment,
    beta_second,
    gain_master,
    gain_moment,
    gain_second,
    learn_rate,
    clip_limit,
):
    proj_local = proj_grads[0, 0]
    beta_local = beta_grads[0, 0]
    gain_local = gain_grads[0, 0, 0]
    micro_count, model_width, columns = proj_local.shape
    heads_here = beta_local.shape[1]
    proj_sum, beta_sum = (
        lax.psum_scatter(
            jnp.sum(proj_local, axis=0, dtype=jnp.float32), "shard", scatter_dimension=0, tiled=True
        ),
        lax.psum_scatter(
            jnp.sum(beta_local, axis=0, dtype=jnp.float32), "shard", scatter_dimension=1, tiled=True
        ),
    )
    local_squares = jnp.sum(proj_sum * proj_sum) + jnp.sum(beta_sum * beta_sum)
    gain_partial = jnp.sum(gain_local, axis=0, dtype=jnp.float32)
    gain_sum = lax.psum_scatter(gain_partial, ("shard", "tensor"), scatter_dimension=0, tiled=True)
    total_squares = lax.psum(
        local_squares + jnp.sum(gain_sum * gain_sum), ("shard", "tensor", "section")
    )
    counted = lax.axis_size("section") * (
        model_width * columns * lax.axis_size("tensor")
        + heads_here * lax.axis_size("tensor") * model_width
        + model_width
    )
    grad_rms = jnp.sqrt(total_squares / counted)
    factor = jnp.minimum(1.0, clip_limit / (jnp.sqrt(total_squares) + norm_eps))
    proj_new = adam_update(
        proj_sum, factor, learn_rate, proj_master[0], proj_moment[0], proj_second[0]
    )
    beta_new = adam_update(
        beta_sum, factor, learn_rate, beta_master[0], beta_moment[0], beta_second[0]
    )
    gain_new = adam_update(
        gain_sum, factor, learn_rate, gain_master[0], gain_moment[0], gain_second[0]
    )
    proj_weights, beta_weights = (
        lax.all_gather(proj_new[0].astype(jnp.bfloat16), "shard", axis=0, tiled=True),
        lax.all_gather(beta_new[0].astype(jnp.bfloat16), "shard", axis=1, tiled=True),
    )
    gain_weights = lax.all_gather(
        gain_new[0].astype(jnp.bfloat16), ("shard", "tensor"), axis=0, tiled=True
    )
    return (
        proj_weights[None],
        beta_weights[None],
        gain_weights[None],
        proj_new[0][None],
        proj_new[1][None],
        proj_new[2][None],
        beta_new[0][None],
        beta_new[1][None],
        beta_new[2][None],
        gain_new[0][None],
        gain_new[1][None],
        gain_new[2][None],
        grad_rms,
    )


def solution(mesh):
    in_specs = (
        P("section", "shard", None, None, "tensor"),
        P("section", "shard", None, "tensor", None),
        P("section", "shard", "tensor", None, None),
        P("section", "shard", "tensor"),
        P("section", "shard", "tensor"),
        P("section", "shard", "tensor"),
        P("section", "tensor", "shard"),
        P("section", "tensor", "shard"),
        P("section", "tensor", "shard"),
        P("section", ("shard", "tensor")),
        P("section", ("shard", "tensor")),
        P("section", ("shard", "tensor")),
        P(),
        P(),
    )
    out_specs = (
        P("section", None, "tensor"),
        P("section", "tensor", None),
        P("section", None),
        P("section", "shard", "tensor"),
        P("section", "shard", "tensor"),
        P("section", "shard", "tensor"),
        P("section", "tensor", "shard"),
        P("section", "tensor", "shard"),
        P("section", "tensor", "shard"),
        P("section", ("shard", "tensor")),
        P("section", ("shard", "tensor")),
        P("section", ("shard", "tensor")),
        P(),
    )
    return jax.shard_map(
        per_device, mesh=mesh, in_specs=in_specs, out_specs=out_specs, check_vma=False
    )
```

profile of v0, /device:TPU:1, one launch (start us, length us, event | category | flops | bytes accessed | tf_op | source)
XLA Modules:
  0.0 671.6 jit_solution(17313761251123311382)
XLA Ops:
  7.2 0.0 copy-start
  7.2 0.0 reduce-scatter.7.cloned.1.call-start
  7.2 0.9 convert_reduce_fusion.1
  8.2 1.3 copy.29
  9.5 0.0 reduce-scatter.7.cloned.1.call-update
  9.5 0.0 reduce-scatter.5.cloned.1.call-start
  9.6 0.0 copy-done
  9.6 1.7 convert_reduce_fusion
  11.3 0.0 copy-start.8
  11.3 0.0 copy-start.4
  11.3 0.0 copy-start.1
  11.3 0.0 copy-start.2
  11.3 0.0 copy-start.3
  11.3 0.0 copy-start.5
  11.3 0.0 copy-start.6
  11.3 0.0 copy-start.7
  11.3 0.0 copy-start.9
  11.3 0.0 copy-start.10
  11.3 0.0 copy-start.11
  11.3 0.0 reduce-scatter.5.cloned.1.call-update
  11.4 0.0 all-gather.3.cloned.1.call-start
  12.8 0.0 copy-done.8
  12.8 0.6 fusion.10
  14.0 0.0 copy-done.4
  14.1 259.2 %all-reduce.1 = f32[2048]{0:T(1024)S(1)} all-reduce(f32[2048]{0:T(1024)S(1)} %convert_reduce_fusion.2), channel_id=4, replica_groups=mesh['shard'=32,'tensor'=4,'section'=4] {'shard','tensor'}, use_global_device_ids=true, to_apply=%region_7.0.clone | all-reduce | flops 2048 | bytes 16384
  273.3 0.7 multiply_reduce_fusion.2
  273.9 0.0 reduce-scatter.7.cloned.1.call-done
  273.9 0.8 copy.30
  274.8 0.6 multiply_reduce_fusion.1
  275.4 0.0 reduce-scatter.5.cloned.1.call-done
  275.4 1.5 multiply_reduce_fusion
  278.8 104.4 %psum.7 = f32[]{:T(128)} all-reduce(f32[]{:T(128)S(6)} %add.51), channel_id=1, replica_groups=mesh['shard'=32,'tensor'=4,'section'=4] {'shard','tensor','section'}, use_global_device_ids=true, to_apply=%region_9.0 | all-reduce | flops 1 | bytes 8 | tf_op jit(solution)/shard_map/psum | solution.py:55
  383.9 0.0 copy-done.1
  383.9 0.0 copy-done.2
  383.9 0.0 copy-done.3
  384.0 1.6 fusion.9
  385.5 0.0 all-gather.3.cloned.1.call-update
  386.2 0.0 copy-done.5
  386.2 0.0 copy-done.6
  386.2 0.0 copy-done.7
  386.2 0.6 convert_bitcast_fusion
  386.8 29.7 %all-gather = bf16[32,64,4]{1,2,0:T(4,128)(2,1)S(1)} all-gather(bf16[1,64,4]{1,2,0:T(4,128)(2,1)S(1)} %get-tuple-element.17), channel_id=1, replica_groups=mesh['shard'=32,'tensor'=4,'section'=4] {'shard'}, dimensions={0}, use_global_device_ids=true | all-gather | bytes 16896 | tf_op jit(solution)/shard_map/all_gather | solution.py:76
  416.6 0.7 reshape.51
  417.3 0.0 copy-done.9
  417.3 0.0 copy-done.10
  417.3 0.0 copy-done.11
  417.3 0.6 fusion.7
  417.9 0.2 dynamic-update-slice
  418.1 242.3 %all-reduce = bf16[2048]{0:T(1024)(128)(2,1)S(1)} all-reduce(bf16[2048]{0:T(1024)(128)(2,1)S(1)} %dynamic-update-slice), channel_id=1, replica_groups=mesh['shard'=32,'tensor'=4,'section'=4] {'shard','tensor'}, use_global_device_ids=true, to_apply=%add | all-reduce | flops 2048 | bytes 8192
  660.4 0.6 broadcast_in_dim.38
  661.7 0.0 all-gather.3.cloned.1.call-done
  661.7 2.3 copy.35
  (3 shorter events, 0.0 us)
Async XLA Ops:
  7.2 2.4 copy-start
  7.2 266.8 %reduce-scatter.7.cloned.1.call-start = ((), (), s32[]{:S(2)}) async-start(), calls=%async_computation.4 | async-start | bytes 1081344
  9.5 265.9 %reduce-scatter.5.cloned.1.call-start = ((), (), s32[]{:S(2)}) async-start(), calls=%async_computation.2 | async-start | bytes 2162688 | tf_op jit(solution)/shard_map/reduce_scatter | solution.py:45
  11.3 1.5 copy-start.8
  11.3 2.8 copy-start.4
  11.3 372.7 %copy-start.1 = (f32[1,64,256]{2,1,0:T(8,128)S(1)}, f32[1,64,256]{2,1,0:T(8,128)}, u32[]{:S(2)}) copy-start(f32[1,64,256]{2,1,0:T(8,128)} %param.19) | copy-start | bytes 196612
  11.3 372.7 %copy-start.2 = (f32[1,64,256]{2,1,0:T(8,128)S(1)}, f32[1,64,256]{2,1,0:T(8,128)}, u32[]{:S(2)}) copy-start(f32[1,64,256]{2,1,0:T(8,128)} %param.18) | copy-start | bytes 196612
  11.3 372.7 %copy-start.3 = (f32[1,64,256]{2,1,0:T(8,128)S(1)}, f32[1,64,256]{2,1,0:T(8,128)}, u32[]{:S(2)}) copy-start(f32[1,64,256]{2,1,0:T(8,128)} %param.17) | copy-start | bytes 196612
  11.3 374.9 %copy-start.5 = (f32[1,4,64]{2,1,0:T(4,128)S(1)}, f32[1,4,64]{2,1,0:T(4,128)}, u32[]{:S(2)}) copy-start(f32[1,4,64]{2,1,0:T(4,128)} %param.22) | copy-start | bytes 3076
  11.3 374.9 %copy-start.6 = (f32[1,4,64]{2,1,0:T(4,128)S(1)}, f32[1,4,64]{2,1,0:T(4,128)}, u32[]{:S(2)}) copy-start(f32[1,4,64]{2,1,0:T(4,128)} %param.21) | copy-start | bytes 3076
  11.3 374.9 %copy-start.7 = (f32[1,4,64]{2,1,0:T(4,128)S(1)}, f32[1,4,64]{2,1,0:T(4,128)}, u32[]{:S(2)}) copy-start(f32[1,4,64]{2,1,0:T(4,128)} %param.20) | copy-start | bytes 3076
  11.3 406.0 %copy-start.9 = (f32[1,16]{1,0:T(1,128)S(1)}, f32[1,16]{1,0:T(1,128)}, u32[]{:S(2)}) copy-start(f32[1,16]{1,0:T(1,128)} %param.23) | copy-start | bytes 196
  11.3 406.0 %copy-start.10 = (f32[1,16]{1,0:T(1,128)S(1)}, f32[1,16]{1,0:T(1,128)}, u32[]{:S(2)}) copy-start(f32[1,16]{1,0:T(1,128)} %param.24) | copy-start | bytes 196
  11.3 406.0 %copy-start.11 = (f32[1,16]{1,0:T(1,128)S(1)}, f32[1,16]{1,0:T(1,128)}, u32[]{:S(2)}) copy-start(f32[1,16]{1,0:T(1,128)} %param.25) | copy-start | bytes 196
  11.4 650.3 %all-gather.3.cloned.1.call-start = ((), (), s32[]{:S(2)}) async-start(), calls=%async_computation.3 | async-start | bytes 1081344 | tf_op jit(solution)/shard_map/all_gather | solution.py:75
Sparse Core Ops, SparseCore 0:
  11.4 111.6 reduce-scatter.6
  126.1 107.6 reduce-scatter.4
  385.7 63.3 all-gather.2
where the time goes:
time: 676 us; the launch traced here: 672 us
  blocking collectives  636 us (94%)
  between operations  21.1 us (3%)
  other arithmetic  8.15 us (1%)
    unnamed x2, blocking collectives  501 us
    psum x1, blocking collectives, per_device(): lax.psum(local_squares + jnp.sum(gain_sum * gain_sum), ('shard', 'tensor'...  104 us
    all_gather x1, blocking collectives, per_device(): lax.all_gather(beta_new[0].astype(jnp.bfloat16), 'shard', axis=1, tiled=T...  29.7 us
  transfers between devices with their start and end apart: 3, of which 0 were waited for; matrix products, arithmetic and copies ran while one was open for 1% of the time, Pallas kernels for 0%

commit v1 on v0

v1 whole, which is shorter than its diff:
```python
import jax
import jax.numpy as jnp
from jax import lax
from jax.sharding import Mesh
from jax.sharding import PartitionSpec as P

first_beta = 0.9
second_beta = 0.95
decay_rate = 0.1
adam_eps = 1e-08
norm_eps = 1e-06


def adam_update(grad, factor, learn_rate, master, moment, second):
    clipped = grad * factor
    moment_new = first_beta * moment + (1.0 - first_beta) * clipped
    second_new = second_beta * second + (1.0 - second_beta) * clipped * clipped
    master_new = master * (1.0 - learn_rate * decay_rate) - learn_rate * moment_new / (
        jnp.sqrt(second_new) + adam_eps
    )
    return (master_new, moment_new, second_new)


def per_device(
    proj_grads,
    beta_grads,
    gain_grads,
    proj_master,
    proj_moment,
    proj_second,
    beta_master,
    beta_moment,
    beta_second,
    gain_master,
    gain_moment,
    gain_second,
    learn_rate,
    clip_limit,
):
    chips = lax.axis_size("z")
    tensor_size = lax.axis_size("tensor")
    sections = lax.axis_size("section")
    core = lax.axis_index("core")
    tensor = lax.axis_index("tensor")
    section = lax.axis_index("section")
    width = proj_grads.shape[3]
    columns = proj_grads.shape[4]
    heads_here = beta_grads.shape[3]
    own = width // chips // 2
    lanes = 2 * own
    halves = columns // lanes

    proj_sum = jnp.sum(proj_grads[0, 0], axis=0, dtype=jnp.float32)
    beta_sum = jnp.sum(beta_grads[0, 0], axis=0, dtype=jnp.float32)
    gain_sum = jnp.sum(gain_grads[0, 0, 0], axis=0, dtype=jnp.float32)
    proj_blocks = proj_sum.reshape(chips, 2, own, halves, lanes).transpose(1, 0, 3, 2, 4)
    proj_blocks = proj_blocks.reshape(2, chips, halves * own, lanes)
    small = jnp.concatenate(
        [
            beta_sum.reshape(heads_here, chips, lanes).transpose(1, 0, 2),
            gain_sum.reshape(chips, 1, lanes),
            jnp.zeros((chips, 7 - heads_here, lanes), jnp.float32),
        ],
        axis=1,
    )
    packed = jnp.concatenate(
        [proj_blocks, jnp.broadcast_to(small[None], (2,) + small.shape)], axis=2
    )
    by_core = lax.all_to_all(packed, "core", 0, 0)
    by_chip = lax.all_to_all(by_core[0] + by_core[1], "z", 0, 0)
    total = jnp.sum(by_chip, axis=0)
    rows = halves * own
    proj_total = total[:rows].reshape(halves, own, lanes).transpose(1, 0, 2).reshape(own, columns)
    beta_wide = total[rows : rows + heads_here]
    gain_partial = total[rows + heads_here]

    lane = lax.iota(jnp.int32, lanes)
    mine = lane // own == core
    beta_total = lax.dynamic_slice_in_dim(beta_wide, core * own, own, axis=1)
    local_squares = jnp.sum(total[:rows] * total[:rows]) + jnp.sum(
        jnp.where(mine, beta_wide * beta_wide, 0.0)
    )

    share = gain_master.shape[1]
    slot = lane // share == core * tensor_size + tensor
    spread = lambda row: jnp.where(slot, jnp.tile(row[0], lanes // share), 0.0)
    message = jnp.stack(
        [
            gain_partial,
            jnp.full((lanes,), local_squares),
            spread(gain_master),
            spread(gain_moment),
            spread(gain_second),
            jnp.zeros((lanes,), jnp.float32),
            jnp.zeros((lanes,), jnp.float32),
            jnp.zeros((lanes,), jnp.float32),
        ]
    )
    peers = tensor_size * sections
    heard = lax.all_to_all(
        jnp.broadcast_to(message[None], (peers,) + message.shape), ("tensor", "section"), 0, 0
    )
    by_section = jnp.sum(heard.reshape((tensor_size, sections) + message.shape), axis=0)
    shard_squares = jnp.sum(by_section[:, 1, 0]) + jnp.sum(
        jnp.where(mine, by_section[:, 0] * by_section[:, 0], 0.0)
    )
    here = lax.broadcasted_iota(jnp.int32, (sections, 1, 1), 0) == section
    gain_rows = jnp.sum(jnp.where(here, by_section, 0.0), axis=0)

    shards = 2 * chips
    squares = lax.all_to_all(
        jnp.full((shards, 1, lanes), shard_squares), ("z", "core"), 0, 0
    )
    total_squares = jnp.sum(squares[:, 0, 0])
    counted = sections * (
        width * columns * tensor_size + heads_here * tensor_size * width + width
    )
    grad_rms = jnp.sqrt(total_squares / counted)
    factor = jnp.minimum(1.0, clip_limit / (jnp.sqrt(total_squares) + norm_eps))

    proj_new = adam_update(
        proj_total, factor, learn_rate, proj_master[0], proj_moment[0], proj_second[0]
    )
    beta_new = adam_update(
        beta_total, factor, learn_rate, beta_master[0], beta_moment[0], beta_second[0]
    )
    gain_new = adam_update(
        gain_rows[0], factor, learn_rate, gain_rows[2], gain_rows[3], gain_rows[4]
    )
    gain_own = [
        lax.dynamic_slice_in_dim(row, core * own + tensor * share, share)[None] for row in gain_new
    ]

    proj_half = proj_new[0].astype(jnp.bfloat16).reshape(own, halves, lanes).transpose(1, 0, 2)
    beta_half = jnp.where(mine, jnp.tile(beta_new[0].astype(jnp.bfloat16), (1, 2)), 0)
    gain_half = jnp.where(mine, gain_new[0].astype(jnp.bfloat16), 0)[None]
    weights = jnp.concatenate(
        [
            proj_half.reshape(rows, lanes),
            beta_half,
            gain_half,
            jnp.zeros((15 - heads_here, lanes), jnp.bfloat16),
        ],
        axis=0,
    )
    gathered = lax.all_gather(weights, "z", axis=0)
    other = lax.ppermute(gathered, "core", [(0, 1), (1, 0)])
    first = core == 0
    pair = jnp.stack([jnp.where(first, gathered, other), jnp.where(first, other, gathered)], axis=1)
    proj_weights = (
        pair[:, :, :rows]
        .reshape(chips, 2, halves, own, lanes)
        .transpose(0, 1, 3, 2, 4)
        .reshape(width, columns)
    )
    tail = jnp.where(mine, gathered[:, rows:], other[:, rows:])
    beta_weights = tail[:, :heads_here].transpose(1, 0, 2).reshape(heads_here, width)
    gain_weights = tail[:, heads_here].reshape(width)
    return (
        proj_weights[None],
        beta_weights[None],
        gain_weights[None],
        proj_new[0][None],
        proj_new[1][None],
        proj_new[2][None],
        beta_new[0][None],
        beta_new[1][None],
        beta_new[2][None],
        gain_own[0],
        gain_own[1],
        gain_own[2],
        grad_rms,
    )


def solution(mesh):
    shard, tensor, section = mesh.devices.shape
    split = Mesh(
        mesh.devices.reshape(shard // 2, 2, tensor, section), ("z", "core", "tensor", "section")
    )
    shard_axes = ("z", "core")
    all_axes = ("z", "core", "tensor")
    in_specs = (
        P("section", shard_axes, None, None, "tensor"),
        P("section", shard_axes, None, "tensor", None),
        P("section", shard_axes, "tensor", None, None),
        P("section", shard_axes, "tensor"),
        P("section", shard_axes, "tensor"),
        P("section", shard_axes, "tensor"),
        P("section", "tensor", shard_axes),
        P("section", "tensor", shard_axes),
        P("section", "tensor", shard_axes),
        P("section", all_axes),
        P("section", all_axes),
        P("section", all_axes),
        P(),
        P(),
    )
    out_specs = (
        P("section", None, "tensor"),
        P("section", "tensor", None),
        P("section", None),
        P("section", shard_axes, "tensor"),
        P("section", shard_axes, "tensor"),
        P("section", shard_axes, "tensor"),
        P("section", "tensor", shard_axes),
        P("section", "tensor", shard_axes),
        P("section", "tensor", shard_axes),
        P("section", all_axes),
        P("section", all_axes),
        P("section", all_axes),
        P(),
    )
    return jax.shard_map(
        per_device, mesh=split, in_specs=in_specs, out_specs=out_specs, check_vma=False
    )
```

time: 676 us -> 169 us (0.25)
  blocking collectives: 636 us -> 35 us
  waiting for transfers between devices: 0.07 us -> 64.4 us
  starting transfers between devices: 0.12 us -> 41.2 us
  between operations: 21.1 us -> 7.49 us
    unnamed x2 -> x0, blocking collectives: 501 us -> none
    psum x1 -> x0, blocking collectives: 104 us -> none  [per_device(): lax.psum(local_squares + jnp.sum(gain_sum * gain_sum), ('shard', 'tensor'...]
    all_to_all x0 -> x3, waiting for transfers between devices: none -> 64.4 us  [the longest x1 46.3 us: per_device(): by_chip = lax.all_to_all(by_core[0] + by_core[1], 'z', 0, 0)]
    all_to_all x0 -> x3, starting transfers between devices: none -> 31.5 us  [the longest x1 15.1 us: per_device(): lax.all_to_all(jnp.full((shards, 1, lanes), shard_squares), ('z', 'core')...]
    all_to_all x0 -> x1, blocking collectives: none -> 12 us  [per_device(): by_core = lax.all_to_all(packed, 'core', 0, 0)]
    ppermute x0 -> x1, starting transfers between devices: none -> 9.68 us  [per_device(): other = lax.ppermute(gathered, 'core', [(0, 1), (1, 0)])]
    all_gather x1, blocking collectives: 29.7 us -> 22.9 us  [per_device(): gathered = lax.all_gather(weights, 'z', axis=0)]
  transfers between devices with their start and end apart: 3 -> 4, of which waited for: 0 -> 3; matrix products, arithmetic and copies ran while one was open for 1% -> 1% of each run, Pallas kernels for 0% -> 0%
where the time goes in v1:
time: 169 us
  waiting for transfers between devices  64.4 us (38%)
  starting transfers between devices  41.2 us (24%)
  blocking collectives  35 us (21%)
  local copies, waits for them, and re-layouts  10.6 us (6%)
  other arithmetic  9.92 us (6%)
  between operations  7.49 us (4%)
    all_to_all x1, waiting for transfers between devices, per_device(): by_chip = lax.all_to_all(by_core[0] + by_core[1], 'z', 0, 0)  46.3 us
    all_gather x1, blocking collectives, per_device(): gathered = lax.all_gather(weights, 'z', axis=0)  22.9 us
    all_to_all x1, starting transfers between devices, per_device(): lax.all_to_all(jnp.full((shards, 1, lanes), shard_squares), ('z', 'core')...  15.1 us
    all_to_all x1, blocking collectives, per_device(): by_core = lax.all_to_all(packed, 'core', 0, 0)  12 us
    all_to_all x1, waiting for transfers between devices, per_device(): lax.all_to_all(jnp.full((shards, 1, lanes), shard_squares), ('z', 'core')...  11.6 us
    ppermute x1, starting transfers between devices, per_device(): other = lax.ppermute(gathered, 'core', [(0, 1), (1, 0)])  9.68 us
    all_to_all x1, starting transfers between devices, per_device(): by_chip = lax.all_to_all(by_core[0] + by_core[1], 'z', 0, 0)  9.67 us
    all_to_all x1, starting transfers between devices, per_device(): lax.all_to_all(jnp.broadcast_to(message[None], (peers,) + message.shape),...  6.75 us
  transfers between devices with their start and end apart: 4, of which 3 were waited for; matrix products, arithmetic and copies ran while one was open for 1% of the time, Pallas kernels for 0%

profile of v1, /device:TPU:1, one launch (start us, length us, event | category | flops | bytes accessed | tf_op | source)
XLA Modules:
  0.0 168.6 jit_solution(2199373359810774463)
XLA Ops:
  0.6 3.5 %convert_reduce_fusion = f32[2048,256]{1,0:T(8,128)} fusion(bf16[1,1,2,2048,256]{4,3,2,1,0:T(8,128)(2,1)} %param.14), kind=kLoop, calls=%fused_computation | loop fusion | flops 1572864 | bytes 4194304 | tf_op jit(solution)/shard_map/reduce_sum | solution.py:53
  4.2 2.3 %reshape.216 = f32[16,2,64,2,128]{4,3,2,1,0:T(2,128)S(1)} reshape(f32[2048,256]{1,0:T(8,128)} %convert_reduce_fusion) | data formatting | bytes 4194304 | tf_op jit(solution)/shard_map/reshape | solution.py:56
  6.5 0.0 copy-start.3
  6.5 0.0 copy-start.4
  6.5 0.3 copy.49
  6.8 0.5 copy-done.3
  7.2 0.0 copy-done.4
  7.3 0.1 pad.10.clone
  7.4 0.1 maximum_maximum_fusion
  7.5 0.2 pad_maximum_fusion
  7.6 12.0 %all_to_all.20 = f32[2,16,136,128]{3,2,1,0:T(8,128)S(1)} all-to-all(f32[2,16,136,128]{3,2,1,0:T(8,128)S(1)} %pad_maximum_fusion), channel_id=1, replica_groups=mesh['z'=16,'core'=2,'tensor'=4,'section'=4] {'core'}, dimensions={0} | all-to-all | bytes 4456448 | tf_op jit(solution)/shard_map/all_to_all | solution.py:69
  19.7 0.0 copy-start.8
  19.7 0.0 copy-start.9
  19.7 1.1 fusion
  20.8 9.7 %all-to-all-start.1 = ((f32[16,136,128]{2,1,0:T(8,128)}), f32[16,136,128]{2,1,0:T(8,128)S(1)}, u32[]{:S(2)}, u32[]{:S(2)}) async-start(f32[16,136,128]{2,1,0:T(8,128)} %fusion), calls=%async_computation.1 | async-start | bytes 2228224 | tf_op jit(solution)/shard_map/all_to_all | solution.py:70
  30.5 0.0 copy-start.5
  30.5 0.0 copy-start.6
  30.5 0.0 copy-start.7
  30.5 0.0 copy-done.8
  30.5 0.1 tile.44
  30.6 0.0 copy-done.9
  30.6 0.1 tile.47
  30.7 0.0 copy-done.10
  30.7 0.1 tile.41
  32.1 0.1 pad.5.clone
  32.2 46.3 %all-to-all-done.1 = f32[16,136,128]{2,1,0:T(8,128)S(1)} async-done(((f32[16,136,128]{2,1,0:T(8,128)}), f32[16,136,128]{2,1,0:T(8,128)S(1)}, u32[]{:S(2)}, u32[]{:S(2)}) %all-to-all-start.1) | async-done | bytes 1114144 | tf_op jit(solution)/shard_map/all_to_all | solution.py:70
  78.5 0.1 reduce_sum.102
  78.6 0.6 multiply_reduce_fusion
  79.2 0.6 fusion.21
  81.2 0.6 broadcast_in_dim.90
  81.8 6.8 %all-to-all-start.2 = ((f32[16,8,128]{2,1,0:T(8,128)}), f32[16,8,128]{2,1,0:T(8,128)S(1)}, u32[]{:S(2)}, u32[]{:S(2)}) async-start(f32[16,8,128]{2,1,0:T(8,128)} %broadcast_in_dim.90), calls=%async_computation.2 | async-start | bytes 131072 | tf_op jit(solution)/shard_map/all_to_all | solution.py:100
  88.6 6.5 %all-to-all-done.2 = f32[16,8,128]{2,1,0:T(8,128)S(1)} async-done(((f32[16,8,128]{2,1,0:T(8,128)}), f32[16,8,128]{2,1,0:T(8,128)S(1)}, u32[]{:S(2)}, u32[]{:S(2)}) %all-to-all-start.2) | async-done | bytes 65568 | tf_op jit(solution)/shard_map/all_to_all | solution.py:100
  95.1 0.6 slice_reduce_fusion.1
  95.7 0.6 select_reduce_fusion.1
  97.6 0.6 broadcast_in_dim.91
  98.2 15.1 %all-to-all-start.3 = ((f32[32,1,128]{2,1,0:T(1,128)}), f32[32,1,128]{2,1,0:T(1,128)S(1)}, u32[]{:S(2)}, u32[]{:S(2)}) async-start(f32[32,1,128]{2,1,0:T(1,128)} %broadcast_in_dim.91), calls=%async_computation.3 | async-start | bytes 32768 | tf_op jit(solution)/shard_map/all_to_all | solution.py:111
  113.3 0.1 select_reduce_fusion
  113.4 11.6 %all-to-all-done.3 = f32[32,1,128]{2,1,0:T(1,128)S(1)} async-done(((f32[32,1,128]{2,1,0:T(1,128)}), f32[32,1,128]{2,1,0:T(1,128)S(1)}, u32[]{:S(2)}, u32[]{:S(2)}) %all-to-all-start.3) | async-done | bytes 16416 | tf_op jit(solution)/shard_map/all_to_all | solution.py:111
  125.0 0.6 slice_reduce_fusion
  126.4 0.1 copy.55
  126.5 0.1 mul.354
  126.5 0.0 copy-done
  126.5 0.0 copy-done.1
  126.5 0.0 copy-done.2
  126.6 0.7 divide_subtract_fusion
  127.4 0.0 copy-done.5
  127.4 0.0 copy-done.6
  127.4 0.0 copy-done.7
  127.4 0.7 fusion.20
  128.1 0.1 tile.49
  128.2 0.1 fusion.8
  128.3 0.1 maximum_maximum_fusion.1
  128.4 22.9 %all-gather = bf16[2304,128]{1,0:T(8,128)(2,1)S(1)} all-gather(bf16[144,128]{1,0:T(8,128)(2,1)S(1)} %maximum_maximum_fusion.1), channel_id=2, replica_groups=mesh['z'=16,'core'=2,'tensor'=4,'section'=4] {'z'}, dimensions={0}, use_global_device_ids=true | all-gather | bytes 626688 | tf_op jit(solution)/shard_map/all_gather | solution.py:146
  151.3 9.7 %collective-permute-start = (bf16[16,144,128]{2,1,0:T(8,128)(2,1)S(1)}, bf16[16,144,128]{2,1,0:T(8,128)(2,1)S(1)}, u32[]{:S(2)}, u32[]{:S(2)}) collective-permute-start(bf16[16,144,128]{2,1,0:T(8,128)(2,1)S(1)} %bitcast.79), channel_id=1, source_target_pairs={{0,16},{16,0},{1,17},{17,1},{2,18},{18,2},{3,19},{19,3},{4,20},{20... | collective-permute-start | bytes 1769480 | tf_op jit(solution)/shard_map/ppermute | solution.py:147
  161.7 0.6 dynamic-slice_bitcast_fusion
  162.3 0.6 dynamic-slice_bitcast_fusion.1
  162.9 0.6 dynamic-slice_bitcast_fusion.2
  163.4 0.0 collective-permute-done
  163.5 0.6 slice_bitcast_fusion
  164.1 0.6 slice_bitcast_fusion.1
  164.7 0.1 select_bitcast_fusion.1
  164.8 0.1 pad_maximum_fusion.1
  164.9 1.1 copy.54
  166.0 1.5 broadcast_in_dim_reshape.6
  (32 shorter events, 0.3 us)
Async XLA Ops:
  6.5 0.8 copy-start.3
  6.5 0.8 copy-start.4
  19.7 10.8 %copy-start.8 = (f32[1,16]{1,0:T(1,128)S(1)}, f32[1,16]{1,0:T(1,128)}, u32[]{:S(2)}) copy-start(f32[1,16]{1,0:T(1,128)} %param.24) | copy-start | bytes 196
  19.7 10.9 %copy-start.9 = (f32[1,16]{1,0:T(1,128)S(1)}, f32[1,16]{1,0:T(1,128)}, u32[]{:S(2)}) copy-start(f32[1,16]{1,0:T(1,128)} %param.25) | copy-start | bytes 196
  19.7 11.0 %copy-start.10 = (f32[1,16]{1,0:T(1,128)S(1)}, f32[1,16]{1,0:T(1,128)}, u32[]{:S(2)}) copy-start(f32[1,16]{1,0:T(1,128)} %param.23) | copy-start | bytes 196
  20.8 105.8 %copy-start = (f32[1,64,256]{2,1,0:T(8,128)S(1)}, f32[1,64,256]{2,1,0:T(8,128)}, u32[]{:S(2)}) copy-start(f32[1,64,256]{2,1,0:T(8,128)} %param.18) | copy-start | bytes 196612
  20.8 105.8 %copy-start.1 = (f32[1,64,256]{2,1,0:T(8,128)S(1)}, f32[1,64,256]{2,1,0:T(8,128)}, u32[]{:S(2)}) copy-start(f32[1,64,256]{2,1,0:T(8,128)} %param.19) | copy-start | bytes 196612
  20.8 105.8 %copy-start.2 = (f32[1,64,256]{2,1,0:T(8,128)S(1)}, f32[1,64,256]{2,1,0:T(8,128)}, u32[]{:S(2)}) copy-start(f32[1,64,256]{2,1,0:T(8,128)} %param.17) | copy-start | bytes 196612
  20.8 57.7 %all-to-all-start.1 = ((f32[16,136,128]{2,1,0:T(8,128)}), f32[16,136,128]{2,1,0:T(8,128)S(1)}, u32[]{:S(2)}, u32[]{:S(2)}) async-start(f32[16,136,128]{2,1,0:T(8,128)} %fusion), calls=%async_computation.1 | async-start | bytes 2228224 | tf_op jit(solution)/shard_map/all_to_all | solution.py:70
  30.5 96.9 %copy-start.5 = (f32[1,4,64]{2,1,0:T(4,128)S(1)}, f32[1,4,64]{2,1,0:T(4,128)}, u32[]{:S(2)}) copy-start(f32[1,4,64]{2,1,0:T(4,128)} %param.22) | copy-start | bytes 3076
  30.5 96.9 %copy-start.6 = (f32[1,4,64]{2,1,0:T(4,128)S(1)}, f32[1,4,64]{2,1,0:T(4,128)}, u32[]{:S(2)}) copy-start(f32[1,4,64]{2,1,0:T(4,128)} %param.21) | copy-start | bytes 3076
  30.5 96.9 %copy-start.7 = (f32[1,4,64]{2,1,0:T(4,128)S(1)}, f32[1,4,64]{2,1,0:T(4,128)}, u32[]{:S(2)}) copy-start(f32[1,4,64]{2,1,0:T(4,128)} %param.20) | copy-start | bytes 3076
  81.8 13.3 %all-to-all-start.2 = ((f32[16,8,128]{2,1,0:T(8,128)}), f32[16,8,128]{2,1,0:T(8,128)S(1)}, u32[]{:S(2)}, u32[]{:S(2)}) async-start(f32[16,8,128]{2,1,0:T(8,128)} %broadcast_in_dim.90), calls=%async_computation.2 | async-start | bytes 131072 | tf_op jit(solution)/shard_map/all_to_all | solution.py:100
  98.2 26.8 %all-to-all-start.3 = ((f32[32,1,128]{2,1,0:T(1,128)}), f32[32,1,128]{2,1,0:T(1,128)S(1)}, u32[]{:S(2)}, u32[]{:S(2)}) async-start(f32[32,1,128]{2,1,0:T(1,128)} %broadcast_in_dim.91), calls=%async_computation.3 | async-start | bytes 32768 | tf_op jit(solution)/shard_map/all_to_all | solution.py:111
  151.3 12.2 %collective-permute-start = (bf16[16,144,128]{2,1,0:T(8,128)(2,1)S(1)}, bf16[16,144,128]{2,1,0:T(8,128)(2,1)S(1)}, u32[]{:S(2)}, u32[]{:S(2)}) collective-permute-start(bf16[16,144,128]{2,1,0:T(8,128)(2,1)S(1)} %bitcast.79), channel_id=1, source_target_pairs={{0,16},{16,0},{1,17},{17,1},{2,18},{18,2},{3,19},{19,3},{4,20},{20... | collective-permute-start | bytes 1769480 | tf_op jit(solution)/shard_map/ppermute | solution.py:147

commit v2 on v0

v2 whole, which is shorter than its diff:
```python
import jax
import jax.numpy as jnp
from jax import lax
from jax.experimental import pallas as pl
from jax.experimental.pallas import tpu as pltpu
from jax.sharding import PartitionSpec as P

first_beta = 0.9
second_beta = 0.95
decay_rate = 0.1
adam_eps = 1e-08
norm_eps = 1e-06

LANES = 128
TILE = 8
GROUP = 4

VMEM = pl.BlockSpec(memory_space=pltpu.VMEM)
SMEM = pl.BlockSpec(memory_space=pltpu.SMEM)


def adam_update(grad, factor, learn_rate, master, moment, second):
    clipped = grad * factor
    moment_new = first_beta * moment + (1.0 - first_beta) * clipped
    second_new = second_beta * second + (1.0 - second_beta) * clipped * clipped
    master_new = master * (1.0 - learn_rate * decay_rate) - learn_rate * moment_new / (
        jnp.sqrt(second_new) + adam_eps
    )
    return (master_new, moment_new, second_new)


def f32(shape):
    return jax.ShapeDtypeStruct(shape, jnp.float32)


def near_f32(shape):
    return pltpu.VMEM(shape, jnp.float32)


def held(value):
    return pltpu.with_memory_space_constraint(value, pltpu.VMEM)


def pack_kernel(core_ref, proj_ref, beta_ref, gain_ref, out_ref):
    heads_here = beta_ref.shape[1]
    own = proj_ref.shape[3]
    width = beta_ref.shape[2]
    residue = pl.program_id(0)
    tail = jnp.zeros((TILE - heads_here - 1, LANES), jnp.float32)
    for high in range(GROUP):
        rows = proj_ref[0, high, 0].astype(jnp.float32) + proj_ref[1, high, 0].astype(jnp.float32)
        for half in range(rows.shape[1] // LANES):
            out_ref[0, high, half * own : (half + 1) * own, :] = rows[
                :, half * LANES : (half + 1) * LANES
            ]
        start = pl.multiple_of((high * GROUP + residue) * LANES, LANES)
        columns = pl.ds(start, LANES)
        beta = beta_ref[0, :, columns].astype(jnp.float32) + beta_ref[1, :, columns].astype(
            jnp.float32
        )
        gain = gain_ref[:, columns].astype(jnp.float32)
        gain = gain[0:1] + gain[1:2]
        out_ref[0, high, 2 * own :, :] = jnp.concatenate([beta, gain, tail], axis=0)


def pack(which, proj, beta, gain, rows):
    own, columns = proj.shape[3:]
    return pl.pallas_call(
        pack_kernel,
        grid_spec=pltpu.PrefetchScalarGridSpec(
            num_scalar_prefetch=1,
            grid=(GROUP,),
            in_specs=[
                pl.BlockSpec(
                    (2, GROUP, 1, own, columns), lambda i, core: (0, 0, 2 * i + core[0], 0, 0)
                ),
                pl.BlockSpec(beta.shape, lambda i, core: (0, 0, 0)),
                pl.BlockSpec(gain.shape, lambda i, core: (0, 0)),
            ],
            out_specs=pl.BlockSpec((1, GROUP, rows, LANES), lambda i, core: (i, 0, 0, 0)),
        ),
        out_shape=f32((GROUP, GROUP, rows, LANES)),
        name="pack",
    )(which, proj, beta, gain)


def add_kernel(left_ref, right_ref, out_ref):
    out_ref[...] = left_ref[...] + right_ref[...]


def sum_kernel(in_ref, out_ref):
    out_ref[...] = (in_ref[0] + in_ref[1]) + (in_ref[2] + in_ref[3])


def norm_kernel(place_ref, in_ref, master_ref, moment_ref, second_ref, total_ref, message_ref):
    rows = total_ref.shape[0] - TILE
    own = LANES // 2
    heads_here = TILE // 2
    share = master_ref.shape[1]
    core, tensor = place_ref[0], place_ref[1]
    total = (in_ref[0] + in_ref[1]) + (in_ref[2] + in_ref[3])
    total_ref[...] = total
    proj = total[:rows]
    squares = proj * proj
    folded = squares[0:TILE]
    for row in range(TILE, rows, TILE):
        folded = folded + squares[row : row + TILE]
    tail = total[rows:]
    lane = lax.broadcasted_iota(jnp.int32, (TILE, LANES), 1)
    row = lax.broadcasted_iota(jnp.int32, (TILE, LANES), 0)
    mine = (lane // own == core) & (row < heads_here)
    folded = folded + jnp.where(mine, tail * tail, 0.0)
    local = jnp.sum(jnp.sum(folded, axis=0, keepdims=True), axis=1, keepdims=True)
    offset = core * own + tensor * share
    slot_from = lax.broadcasted_iota(jnp.int32, (share, LANES), 0)
    slot_to = lax.broadcasted_iota(jnp.int32, (share, LANES), 1)
    select = jnp.where(slot_from + offset == slot_to, 1.0, 0.0).astype(jnp.float32)
    spread = lambda ref: jnp.dot(
        ref[...], select, precision=lax.Precision.HIGHEST, preferred_element_type=jnp.float32
    )
    message = jnp.concatenate(
        [
            tail[heads_here : heads_here + 1],
            jnp.broadcast_to(local, (1, LANES)),
            spread(master_ref),
            spread(moment_ref),
            spread(second_ref),
            jnp.zeros((TILE - 5, LANES), jnp.float32),
        ],
        axis=0,
    )
    for peer in range(message_ref.shape[0]):
        message_ref[peer] = message


def section_kernel(place_ref, heard_ref, gain_ref, message_ref):
    core, section = place_ref[0], place_ref[2]
    own = LANES // 2
    sections = heard_ref.shape[0] // GROUP
    lane = lax.broadcasted_iota(jnp.int32, (TILE, LANES), 1)
    row = lax.broadcasted_iota(jnp.int32, (TILE, LANES), 0)
    mine = (lane // own == core) & (row == 0)
    counted = jnp.zeros((TILE, LANES), jnp.float32)
    here = jnp.zeros((TILE, LANES), jnp.float32)
    for other in range(sections):
        rows = heard_ref[other]
        for rank in range(1, GROUP):
            rows = rows + heard_ref[rank * sections + other]
        counted = counted + jnp.where(mine, rows * rows, 0.0)
        counted = counted + jnp.where((row == 1) & (lane == 0), rows, 0.0)
        here = here + jnp.where(section == other, rows, 0.0)
    gain_ref[...] = here
    total = jnp.sum(jnp.sum(counted, axis=0, keepdims=True), axis=1, keepdims=True)
    message_ref[...] = jnp.broadcast_to(total.reshape(1, 1, 1), message_ref.shape)


def update_kernel(
    place_ref,
    scalars_ref,
    squares_ref,
    total_ref,
    gain_ref,
    proj_master_ref,
    proj_moment_ref,
    proj_second_ref,
    beta_master_ref,
    beta_moment_ref,
    beta_second_ref,
    weights_ref,
    proj_master_out,
    proj_moment_out,
    proj_second_out,
    beta_master_out,
    beta_moment_out,
    beta_second_out,
    gain_master_out,
    gain_moment_out,
    gain_second_out,
    rms_ref,
    *,
    counted,
):
    core, tensor = place_ref[0], place_ref[1]
    own = proj_master_ref.shape[0]
    heads_here = beta_master_ref.shape[0]
    share = gain_master_out.shape[1]
    rows = total_ref.shape[0] - TILE
    rate = scalars_ref[0]
    squares = jnp.sum(squares_ref[...], axis=0)
    rms_ref[...] = jnp.sqrt(squares / counted)
    factor = jnp.minimum(1.0, scalars_ref[1] / (jnp.sqrt(squares) + norm_eps))
    for half in range(rows // own):
        columns = slice(half * LANES, (half + 1) * LANES)
        block = slice(half * own, (half + 1) * own)
        master, moment, second = adam_update(
            total_ref[block, :],
            factor,
            rate,
            proj_master_ref[:, columns],
            proj_moment_ref[:, columns],
            proj_second_ref[:, columns],
        )
        proj_master_out[:, columns] = master
        proj_moment_out[:, columns] = moment
        proj_second_out[:, columns] = second
        weights_ref[block, :] = master.astype(jnp.bfloat16)
    tail = pltpu.roll(total_ref[rows:, :], LANES - core * own, 1)
    beta = adam_update(
        tail[:heads_here, :own],
        factor[:, :own],
        rate,
        beta_master_ref[...],
        beta_moment_ref[...],
        beta_second_ref[...],
    )
    beta_master_out[...] = beta[0]
    beta_moment_out[...] = beta[1]
    beta_second_out[...] = beta[2]
    gain = adam_update(
        gain_ref[0:1], factor, rate, gain_ref[2:3], gain_ref[3:4], gain_ref[4:5]
    )
    stacked = jnp.concatenate(list(gain) + [jnp.zeros((TILE - 3, LANES), jnp.float32)], axis=0)
    rolled = pltpu.roll(stacked, LANES - core * own - tensor * share, 1)
    gain_master_out[...] = rolled[0:1, :share]
    gain_moment_out[...] = rolled[1:2, :share]
    gain_second_out[...] = rolled[2:3, :share]
    both = jnp.concatenate([beta[0], beta[0]], axis=1)
    weights_ref[rows:, :] = jnp.concatenate(
        [both, gain[0], jnp.zeros((2 * TILE - heads_here - 1, LANES), jnp.float32)], axis=0
    ).astype(jnp.bfloat16)


def spread_kernel(core_ref, mine_ref, other_ref, proj_ref, beta_ref, gain_ref):
    core = core_ref[0]
    chips = mine_ref.shape[0]
    own, columns = proj_ref.shape[2:]
    heads_here = beta_ref.shape[0]
    rows = own * (columns // LANES)
    lane = lax.broadcasted_iota(jnp.int32, (2 * TILE, LANES), 1)
    keep = lane // (LANES // 2) == core
    for chip in range(chips):
        for half in range(columns // LANES):
            block = slice(half * own, (half + 1) * own)
            lanes = slice(half * LANES, (half + 1) * LANES)
            proj_ref[chip, core, :, lanes] = mine_ref[chip, block, :]
            proj_ref[chip, 1 - core, :, lanes] = other_ref[chip, block, :]
        tail = jnp.where(
            keep,
            mine_ref[chip, rows:, :].astype(jnp.float32),
            other_ref[chip, rows:, :].astype(jnp.float32),
        ).astype(jnp.bfloat16)
        lanes = slice(chip * LANES, (chip + 1) * LANES)
        beta_ref[:, lanes] = tail[:heads_here]
        gain_ref[:, lanes] = tail[heads_here : heads_here + 1]


def per_device(
    proj_grads,
    beta_grads,
    gain_grads,
    proj_master,
    proj_moment,
    proj_second,
    beta_master,
    beta_moment,
    beta_second,
    gain_master,
    gain_moment,
    gain_second,
    learn_rate,
    clip_limit,
):
    shards = lax.axis_size("shard")
    tensor_size = lax.axis_size("tensor")
    sections = lax.axis_size("section")
    chips = shards // 2
    micro, width, columns = proj_grads.shape[2:]
    heads_here = beta_grads.shape[3]
    own = width // shards
    rows = own * (columns // LANES)
    core = lax.axis_index("shard") % 2
    place = jnp.stack([core, lax.axis_index("tensor"), lax.axis_index("section")]).astype(jnp.int32)

    core_pairs = [(s, s ^ 1) for s in range(shards)]
    near = []
    for side in range(2):
        for base in range(0, chips, GROUP):
            members = [(base + 2 * side + j) % chips for j in range(GROUP)]
            near.append([2 * z + side for z in sorted(members, key=lambda z: z % GROUP)])
    far = [
        [2 * (residue + high * GROUP) + side for high in range(chips // GROUP)]
        for side in range(2)
        for residue in range(GROUP)
    ]

    proj = proj_grads[0, 0].reshape(micro, chips // GROUP, 2 * GROUP, own, columns)
    beta = beta_grads[0, 0]
    gain = gain_grads[0, 0, 0]
    send = pack(1 - place[0:1], proj, beta, gain, rows + TILE)
    kept = pack(place[0:1], proj, beta, gain, rows + TILE)
    got = lax.ppermute(send, "shard", core_pairs)
    chip_sum = pl.pallas_call(
        add_kernel,
        out_shape=near_f32(kept.shape),
        in_specs=[VMEM, VMEM],
        out_specs=VMEM,
        name="core_add",
    )(kept, held(got))
    scalars = jnp.stack([learn_rate, clip_limit])
    chip_sum, place, scalars = lax.optimization_barrier((chip_sum, place, scalars))
    by_near = lax.all_to_all(chip_sum, "shard", 0, 0, axis_index_groups=near)
    near_sum = pl.pallas_call(
        sum_kernel, out_shape=near_f32(by_near.shape[1:]), in_specs=[VMEM], out_specs=VMEM, name="near"
    )(held(by_near))
    by_far = lax.all_to_all(near_sum, "shard", 0, 0, axis_index_groups=far)
    peers = tensor_size * sections
    total, message = pl.pallas_call(
        norm_kernel,
        out_shape=(near_f32((rows + TILE, LANES)), near_f32((peers, TILE, LANES))),
        in_specs=[SMEM] + [VMEM] * 4,
        out_specs=(VMEM, VMEM),
        name="norm",
    )(place, held(by_far), gain_master, gain_moment, gain_second)
    heard = lax.all_to_all(message, ("tensor", "section"), 0, 0)
    gain_rows, squares = pl.pallas_call(
        section_kernel,
        out_shape=(near_f32((TILE, LANES)), near_f32((shards, 1, LANES))),
        in_specs=[SMEM, VMEM],
        out_specs=(VMEM, VMEM),
        name="section",
    )(place, held(heard))
    squares = lax.all_to_all(squares, "shard", 0, 0)
    counted = sections * (
        width * columns * tensor_size + heads_here * tensor_size * width + width
    )
    state = f32((own, columns))
    beta_state = f32((heads_here, own))
    gain_state = f32(gain_master.shape)
    outs = pl.pallas_call(
        lambda *refs: update_kernel(*refs, counted=float(counted)),
        out_shape=(pltpu.VMEM((rows + 2 * TILE, LANES), jnp.bfloat16),)
        + (state,) * 3
        + (beta_state,) * 3
        + (gain_state,) * 3
        + (f32((1, LANES)),),
        in_specs=[SMEM] * 2 + [VMEM] * 9,
        out_specs=(VMEM,) * 11,
        name="update",
    )(
        place,
        scalars,
        held(squares),
        held(total),
        held(gain_rows),
        proj_master[0],
        proj_moment[0],
        proj_second[0],
        beta_master[0],
        beta_moment[0],
        beta_second[0],
    )
    z_groups = [[2 * z + side for z in range(chips)] for side in range(2)]
    gathered = lax.all_gather(outs[0], "shard", axis=0, axis_index_groups=z_groups)
    other = lax.ppermute(gathered, "shard", core_pairs)
    proj_weights, beta_weights, gain_weights = pl.pallas_call(
        spread_kernel,
        out_shape=(
            jax.ShapeDtypeStruct((chips, 2, own, columns), jnp.bfloat16),
            jax.ShapeDtypeStruct((heads_here, width), jnp.bfloat16),
            jax.ShapeDtypeStruct((1, width), jnp.bfloat16),
        ),
        in_specs=[SMEM, VMEM, VMEM],
        out_specs=(VMEM,) * 3,
        name="spread",
    )(place, held(gathered), held(other))
    return (
        proj_weights.reshape(1, width, columns),
        beta_weights[None],
        gain_weights,
        outs[1][None],
        outs[2][None],
        outs[3][None],
        outs[4][None],
        outs[5][None],
        outs[6][None],
        outs[7],
        outs[8],
        outs[9],
        outs[10][0, 0],
    )


def solution(mesh):
    in_specs = (
        P("section", "shard", None, None, "tensor"),
        P("section", "shard", None, "tensor", None),
        P("section", "shard", "tensor", None, None),
        P("section", "shard", "tensor"),
        P("section", "shard", "tensor"),
        P("section", "shard", "tensor"),
        P("section", "tensor", "shard"),
        P("section", "tensor", "shard"),
        P("section", "tensor", "shard"),
        P("section", ("shard", "tensor")),
        P("section", ("shard", "tensor")),
        P("section", ("shard", "tensor")),
        P(),
        P(),
    )
    out_specs = (
        P("section", None, "tensor"),
        P("section", "tensor", None),
        P("section", None),
        P("section", "shard", "tensor"),
        P("section", "shard", "tensor"),
        P("section", "shard", "tensor"),
        P("section", "tensor", "shard"),
        P("section", "tensor", "shard"),
        P("section", "tensor", "shard"),
        P("section", ("shard", "tensor")),
        P("section", ("shard", "tensor")),
        P("section", ("shard", "tensor")),
        P(),
    )
    return jax.shard_map(
        per_device, mesh=mesh, in_specs=in_specs, out_specs=out_specs, check_vma=False
    )
```

time: 676 us -> 146 us (0.22)
  blocking collectives: 636 us -> 108 us
  between operations: 21.1 us -> 1.99 us
  starting transfers between devices: 0.12 us -> 18.5 us
  Pallas kernels: 0 us -> 13.6 us
  other arithmetic: 8.15 us -> 1.2 us
    unnamed x2 -> x0, blocking collectives: 501 us -> none
    psum x1 -> x0, blocking collectives: 104 us -> none  [per_device(): lax.psum(local_squares + jnp.sum(gain_sum * gain_sum), ('shard', 'tensor'...]
    all_to_all x0 -> x4, blocking collectives: none -> 85.3 us  [the longest x1 27.9 us: per_device(): by_near = lax.all_to_all(chip_sum, 'shard', 0, 0, axis_index_groups=near)]
    ppermute x0 -> x2, starting transfers between devices: none -> 18.5 us  [the longest x1 9.68 us: per_device(): other = lax.ppermute(gathered, 'shard', core_pairs)]
    pallas_call x0 -> x8, Pallas kernels: none -> 13.6 us  [the longest x2 6.91 us: pack(): pl.pallas_call(pack_kernel, grid_spec=pltpu.PrefetchScalarGridSpec(num_sc...]
    all_gather x1, blocking collectives: 29.7 us -> 22.9 us  [per_device(): lax.all_gather(outs[0], 'shard', axis=0, axis_index_groups=z_groups)]
  transfers between devices with their start and end apart: 3 -> 2, of which waited for: 0 -> 1; matrix products, arithmetic and copies ran while one was open for 1% -> 1% of each run, Pallas kernels for 0% -> 2%
where the time goes in v2:
time: 146 us; the launch traced here: 145 us
  blocking collectives  108 us (74%)
  starting transfers between devices  18.5 us (13%)
  Pallas kernels  13.6 us (9%)
  between operations  1.99 us (1%)
  waiting for transfers between devices  1.61 us (1%)
    all_to_all x1, blocking collectives, per_device(): by_near = lax.all_to_all(chip_sum, 'shard', 0, 0, axis_index_groups=near)  27.9 us
    all_to_all x1, blocking collectives, per_device(): squares = lax.all_to_all(squares, 'shard', 0, 0)  25.3 us
    all_gather x1, blocking collectives, per_device(): lax.all_gather(outs[0], 'shard', axis=0, axis_index_groups=z_groups)  22.9 us
    all_to_all x1, blocking collectives, per_device(): by_far = lax.all_to_all(near_sum, 'shard', 0, 0, axis_index_groups=far)  19 us
    all_to_all x1, blocking collectives, per_device(): heard = lax.all_to_all(message, ('tensor', 'section'), 0, 0)  13.1 us
    ppermute x1, starting transfers between devices, per_device(): other = lax.ppermute(gathered, 'shard', core_pairs)  9.68 us
    ppermute x1, starting transfers between devices, per_device(): got = lax.ppermute(send, 'shard', core_pairs)  8.77 us
    pallas_call x2, Pallas kernels, pack(): pl.pallas_call(pack_kernel, grid_spec=pltpu.PrefetchScalarGridSpec(num_sc...  6.91 us
  transfers between devices with their start and end apart: 2, of which 1 were waited for; matrix products, arithmetic and copies ran while one was open for 1% of the time, Pallas kernels for 2%

profile of v2, /device:TPU:1, one launch (start us, length us, event | category | flops | bytes accessed | tf_op | source)
XLA Modules:
  0.0 145.0 jit_solution(16238819294097466480)
XLA Ops:
  0.7 3.5 %pack.3 = f32[4,4,136,128]{3,2,1,0:T(8,128)} custom-call(s32[1]{0:T(128)S(6)} %sub.3.core_ref, bf16[2,4,8,64,256]{4,3,2,1,0:T(8,128)(2,1)} %bitcast.29, bf16[2,4,2048]{2,1,0:T(4,128)(2,1)} %bitcast.31, bf16[2,2048]{1,0:T(2,128)(2,1)} %bitcast.36), custom_call_target="tpu_custom_call" | custom-call | tf_op jit(solution)/shard_map/pack/pallas_call | solution.py:68
  4.1 8.8 %collective-permute-start = (f32[4,4,136,128]{3,2,1,0:T(8,128)}, f32[4,4,136,128]{3,2,1,0:T(8,128)S(1)}, u32[]{:S(2)}, u32[]{:S(2)}) collective-permute-start(f32[4,4,136,128]{3,2,1,0:T(8,128)} %pack.3), channel_id=1, source_target_pairs={{0,16},{16,0},{32,48},{48,32},{64,80},{80,64},{96,112},{112,96},{1... | collective-permute-start | bytes 3342344 | tf_op jit(solution)/shard_map/ppermute | solution.py:301
  12.9 3.4 %pack.2.left_ref = f32[4,4,136,128]{3,2,1,0:T(8,128)} custom-call(s32[1]{0:T(128)} %bitcast.core_ref, bf16[2,4,8,64,256]{4,3,2,1,0:T(8,128)(2,1)} %bitcast.30, bf16[2,4,2048]{2,1,0:T(4,128)(2,1)} %bitcast.32, bf16[2,2048]{1,0:T(2,128)(2,1)} %bitcast.37), custom_call_target="tpu_custom_call" | custom-call | tf_op jit(solution)/shard_map/pack/pallas_call | solution.py:68
  17.6 0.6 pad_add_fusion.place_ref.refs_0_.core_ref
  18.3 0.6 pad_maximum_fusion.refs_1_
  18.8 0.0 collective-permute-done.right_ref
  18.8 1.4 core_add.1
  20.2 27.9 %all_to_all.20.in_ref = f32[4,4,136,128]{3,2,1,0:T(8,128)S(1)} all-to-all(f32[4,4,136,128]{3,2,1,0:T(8,128)S(1)} %core_add.1), channel_id=1, replica_groups={{0,32,64,96},{128,160,192,224},{256,288,320,352},{384,416,448,480},{144..., dimensions={0} | all-to-all | bytes 2228224 | tf_op jit(solution)/shard_map/all_to_all | solution.py:311
  48.1 0.1 near.1
  48.2 19.0 %all_to_all.21.in_ref = f32[4,136,128]{2,1,0:T(8,128)S(1)} all-to-all(f32[4,136,128]{2,1,0:T(8,128)S(1)} %near.1), channel_id=1, replica_groups={{0,128,256,384},{32,160,288,416},{64,192,320,448},{96,224,352,480},{16,..., dimensions={0} | all-to-all | bytes 557056 | tf_op jit(solution)/shard_map/all_to_all | solution.py:315
  67.2 1.0 norm.1
  68.1 13.1 %all_to_all.22.heard_ref = f32[16,8,128]{2,1,0:T(8,128)S(1)} all-to-all(f32[16,8,128]{2,1,0:T(8,128)S(1)} %get-tuple-element.37), channel_id=1, replica_groups=mesh['shard'=32,'tensor'=4,'section'=4] {'tensor','section'}, dimensions={0} | all-to-all | bytes 131072 | tf_op jit(solution)/shard_map/all_to_all | solution.py:324
  81.2 0.8 section.1
  82.0 25.3 %all_to_all.23.refs_2_ = f32[32,1,128]{2,1,0:T(1,128)S(1)} all-to-all(f32[32,1,128]{2,1,0:T(1,128)S(1)} %get-tuple-element.38), channel_id=1, replica_groups=mesh['shard'=32,'tensor'=4,'section'=4] {'shard'}, dimensions={0} | all-to-all | bytes 32768 | tf_op jit(solution)/shard_map/all_to_all | solution.py:332
  107.3 1.7 %update.1 = (bf16[144,128]{1,0:T(8,128)(2,1)S(1)}, f32[64,256]{1,0:T(8,128)}, f32[64,256]{1,0:T(8,128)}, f32[64,256]{1,0:T(8,128)}, f32[4,64]{1,0:T(4,128)}, /*i...) custom-call(s32[3]{0:T(128)} %pad_add_fusion.place_ref.refs_0_.core_, ...), custom_call_target="tpu_custom_call" | custom-call | tf_op jit(solution)/shard_map/update/pallas_call | solution.py:339
  109.0 22.9 %all-gather = bf16[2304,128]{1,0:T(8,128)(2,1)S(1)} all-gather(bf16[144,128]{1,0:T(8,128)(2,1)S(1)} %get-tuple-element.41), channel_id=2, replica_groups={{0,32,64,96,128,160,192,224,256,288,320,352,384,416,448,480},{16,48,80,..., dimensions={0}, use_global_device_ids=true | all-gather | bytes 626688 | tf_op jit(solution)/shard_map/all_gather | solution.py:363
  131.9 9.7 %collective-permute-start.1 = (bf16[16,144,128]{2,1,0:T(8,128)(2,1)S(1)}, bf16[16,144,128]{2,1,0:T(8,128)(2,1)S(1)}, u32[]{:S(2)}, u32[]{:S(2)}) collective-permute-start(bf16[16,144,128]{2,1,0:T(8,128)(2,1)S(1)} %bitcast.27), channel_id=1, source_target_pairs={{0,16},{16,0},{32,48},{48,32},{64,80},{80,64},{96,112},{112,96},{1... | collective-permute-start | bytes 1769480 | tf_op jit(solution)/shard_map/ppermute | solution.py:364
  141.6 1.6 %collective-permute-done.1.other_ref = bf16[16,144,128]{2,1,0:T(8,128)(2,1)S(1)} collective-permute-done((bf16[16,144,128]{2,1,0:T(8,128)(2,1)S(1)}, bf16[16,144,128]{2,1,0:T(8,128)(2,1)S(1)}, u32[]{:S(2)}, u32[]{:S(2)}) %collective-permute-start.1) | collective-permute-done | bytes 589856 | tf_op jit(solution)/shard_map/ppermute | solution.py:364
  143.2 1.8 %spread.1 = (bf16[16,2,64,256]{3,2,1,0:T(8,128)(2,1)}, bf16[4,2048]{1,0:T(4,128)(2,1)}, bf16[1,2048]{1,0:T(2,128)(2,1)}) custom-call(s32[3]{0:T(128)} %pad_add_fusion.place_ref.refs_0_.core_ref, bf16[16,144,128]{2,1,0:T(8,128)(2,1)S(1)} %bitcast.28, bf16[16,144,128]{2,1,0:T(8,128)(2,1)S(1)} %collective-permute-done.1.other_ref), custom_call_target="tpu_custom_call" | custom-call | tf_op jit(solution)/shard_map/spread/pallas_call | solution.py:365
Async XLA Ops:
  4.1 14.7 %collective-permute-start = (f32[4,4,136,128]{3,2,1,0:T(8,128)}, f32[4,4,136,128]{3,2,1,0:T(8,128)S(1)}, u32[]{:S(2)}, u32[]{:S(2)}) collective-permute-start(f32[4,4,136,128]{3,2,1,0:T(8,128)} %pack.3), channel_id=1, source_target_pairs={{0,16},{16,0},{32,48},{48,32},{64,80},{80,64},{96,112},{112,96},{1... | collective-permute-start | bytes 3342344 | tf_op jit(solution)/shard_map/ppermute | solution.py:301
  131.9 11.3 %collective-permute-start.1 = (bf16[16,144,128]{2,1,0:T(8,128)(2,1)S(1)}, bf16[16,144,128]{2,1,0:T(8,128)(2,1)S(1)}, u32[]{:S(2)}, u32[]{:S(2)}) collective-permute-start(bf16[16,144,128]{2,1,0:T(8,128)(2,1)S(1)} %bitcast.27), channel_id=1, source_target_pairs={{0,16},{16,0},{32,48},{48,32},{64,80},{80,64},{96,112},{112,96},{1... | collective-permute-start | bytes 1769480 | tf_op jit(solution)/shard_map/ppermute | solution.py:364

commit v3 on v2

v3 whole, which is shorter than its diff:
```python
import functools

import jax
import jax.numpy as jnp
from jax import lax
from jax.experimental import pallas as pl
from jax.experimental.pallas import tpu as pltpu
from jax.sharding import PartitionSpec as P

first_beta = 0.9
second_beta = 0.95
decay_rate = 0.1
adam_eps = 1e-08
norm_eps = 1e-06

LANES = 128
TILE = 8
GROUP = 4
WIRE = jnp.float16
WIRE_SCALE = 2.0**15

VMEM = pl.BlockSpec(memory_space=pltpu.VMEM)
SMEM = pl.BlockSpec(memory_space=pltpu.SMEM)


def adam_update(grad, factor, learn_rate, master, moment, second):
    clipped = grad * factor
    moment_new = first_beta * moment + (1.0 - first_beta) * clipped
    second_new = second_beta * second + (1.0 - second_beta) * clipped * clipped
    master_new = master * (1.0 - learn_rate * decay_rate) - learn_rate * moment_new / (
        jnp.sqrt(second_new) + adam_eps
    )
    return (master_new, moment_new, second_new)


def f32(shape):
    return jax.ShapeDtypeStruct(shape, jnp.float32)


def near_f32(shape):
    return pltpu.VMEM(shape, jnp.float32)


def held(value):
    return pltpu.with_memory_space_constraint(value, pltpu.VMEM)


def pack_kernel(rate_ref, clip_ref, proj_ref, beta_ref, gain_ref, out_ref, scalars_ref, buffer, arrived, *, flip):
    heads_here = beta_ref.shape[1]
    own = proj_ref.shape[3]
    core = lax.axis_index("shard") % 2
    which = 1 - core if flip else core
    copies = [
        pltpu.make_async_copy(
            proj_ref.at[:, :, 2 * residue + which], buffer.at[residue], arrived.at[residue]
        )
        for residue in range(GROUP)
    ]
    for copy in copies:
        copy.start()
    lane = lax.broadcasted_iota(jnp.int32, scalars_ref.shape, 0)
    scalars_ref[...] = jnp.where(lane == 0, rate_ref[0], clip_ref[0])
    beta = beta_ref[0].astype(jnp.float32) + beta_ref[1].astype(jnp.float32)
    gain = gain_ref[...].astype(jnp.float32)
    gain = gain[0:1] + gain[1:2]
    blank = jnp.zeros((TILE - heads_here - 1, LANES), jnp.float32)
    for chip in range(GROUP * GROUP):
        columns = slice(chip * LANES, (chip + 1) * LANES)
        out_ref[chip % GROUP, chip // GROUP, 2 * own :, :] = jnp.concatenate(
            [beta[:, columns], gain[:, columns], blank], axis=0
        )
    for residue in range(GROUP):
        copies[residue].wait()
        for high in range(GROUP):
            rows = buffer[residue, 0, high].astype(jnp.float32) + buffer[residue, 1, high].astype(
                jnp.float32
            )
            for half in range(rows.shape[1] // LANES):
                out_ref[residue, high, half * own : (half + 1) * own, :] = rows[
                    :, half * LANES : (half + 1) * LANES
                ]


def pack(flip, rate, clip, proj, beta, gain, rows):
    own, columns = proj.shape[3:]
    return pl.pallas_call(
        functools.partial(pack_kernel, flip=flip),
        in_specs=[SMEM, SMEM, pl.BlockSpec(memory_space=pl.ANY), VMEM, VMEM],
        out_specs=(VMEM, VMEM),
        out_shape=(f32((GROUP, GROUP, rows, LANES)), near_f32((TILE, LANES))),
        scratch_shapes=[
            pltpu.VMEM((GROUP, 2, GROUP, own, columns), jnp.bfloat16),
            pltpu.SemaphoreType.DMA((GROUP,)),
        ],
        name="pack",
    )(rate, clip, proj, beta, gain)


def add_kernel(left_ref, right_ref, out_ref):
    out_ref[...] = left_ref[...] + right_ref[...]


def sum_kernel(in_ref, out_ref):
    out_ref[...] = (in_ref[0] + in_ref[1]) + (in_ref[2] + in_ref[3])


def norm_kernel(in_ref, master_ref, moment_ref, second_ref, total_ref, message_ref):
    rows = total_ref.shape[0] - TILE
    own = LANES // 2
    heads_here = TILE // 2
    share = master_ref.shape[1]
    core = lax.axis_index("shard") % 2
    total = (in_ref[0] + in_ref[1]) + (in_ref[2] + in_ref[3])
    tail = pltpu.roll(total[rows:], LANES - core * own, 1)
    total_ref[:rows, :] = total[:rows]
    total_ref[rows:, :] = tail
    squares = total[:rows] * total[:rows]
    folded = squares[0:TILE]
    for row in range(TILE, rows, TILE):
        folded = folded + squares[row : row + TILE]
    lane = lax.broadcasted_iota(jnp.int32, (TILE, LANES), 1)
    row = lax.broadcasted_iota(jnp.int32, (TILE, LANES), 0)
    folded = folded + jnp.where((lane < own) & (row < heads_here), tail * tail, 0.0)
    local = jnp.sum(jnp.sum(folded, axis=0, keepdims=True), axis=1, keepdims=True)
    state = jnp.concatenate(
        [
            jnp.zeros((1, LANES - 3 * share), jnp.float32),
            master_ref[...],
            moment_ref[...],
            second_ref[...],
        ],
        axis=1,
    )
    lane = lane[0:1]
    message = jnp.where(
        lane < own,
        tail[heads_here : heads_here + 1],
        jnp.where(lane == own, local, state),
    )
    for peer in range(message_ref.shape[0]):
        message_ref[peer] = message


def section_kernel(heard_ref, gain_ref, message_ref):
    section = lax.axis_index("section")
    own = LANES // 2
    sections = heard_ref.shape[0] // GROUP
    share = own // GROUP
    lane = lax.broadcasted_iota(jnp.int32, (1, LANES), 1)
    counted = jnp.zeros((1, LANES), jnp.float32)
    here = jnp.zeros((1, LANES), jnp.float32)
    ranks = [jnp.zeros((1, LANES), jnp.float32) for _ in range(GROUP)]
    for other in range(sections):
        rows = [heard_ref[rank * sections + other] for rank in range(GROUP)]
        summed = (rows[0] + rows[1]) + (rows[2] + rows[3])
        counted = counted + jnp.where(
            lane < own, summed * summed, jnp.where(lane == own, summed, 0.0)
        )
        here = here + jnp.where(section == other, summed, 0.0)
        ranks = [
            rank + jnp.where(section == other, row, 0.0) for rank, row in zip(ranks, rows)
        ]
    gain_ref[0:1, :] = here
    for kind in range(3):
        start = LANES - (3 - kind) * share
        state = jnp.ones((1, LANES), jnp.float32)
        for rank in range(GROUP):
            moved = pltpu.roll(ranks[rank], (rank * share - start) % LANES, 1)
            state = jnp.where(lane // share == rank, moved, state)
        gain_ref[kind + 1 : kind + 2, :] = state
    gain_ref[4:, :] = jnp.zeros((TILE - 4, LANES), jnp.float32)
    total = jnp.broadcast_to(jnp.sum(counted, axis=1, keepdims=True), (1, LANES))
    for peer in range(message_ref.shape[0]):
        message_ref[peer] = total


def update_kernel(
    scalars_ref,
    squares_ref,
    total_ref,
    gain_ref,
    proj_master_ref,
    proj_moment_ref,
    proj_second_ref,
    beta_master_ref,
    beta_moment_ref,
    beta_second_ref,
    weights_ref,
    proj_master_out,
    proj_moment_out,
    proj_second_out,
    beta_master_out,
    beta_moment_out,
    beta_second_out,
    gain_master_out,
    gain_moment_out,
    gain_second_out,
    rms_ref,
    *,
    counted,
):
    core, tensor = lax.axis_index("shard") % 2, lax.axis_index("tensor")
    own = proj_master_ref.shape[0]
    heads_here = beta_master_ref.shape[0]
    share = gain_master_out.shape[1]
    rows = total_ref.shape[0] - TILE
    rate = scalars_ref[0:1, :]
    squares = jnp.sum(squares_ref[...], axis=0)
    rms_ref[...] = jnp.sqrt(squares / counted)
    factor = jnp.minimum(1.0, scalars_ref[1:2, :] / (jnp.sqrt(squares) + norm_eps))
    for half in range(rows // own):
        columns = slice(half * LANES, (half + 1) * LANES)
        block = slice(half * own, (half + 1) * own)
        master, moment, second = adam_update(
            total_ref[block, :],
            factor,
            rate,
            proj_master_ref[:, columns],
            proj_moment_ref[:, columns],
            proj_second_ref[:, columns],
        )
        proj_master_out[:, columns] = master
        proj_moment_out[:, columns] = moment
        proj_second_out[:, columns] = second
        weights_ref[:own, columns] = master.astype(jnp.bfloat16)
    beta = adam_update(
        total_ref[rows : rows + heads_here, :own],
        factor[:, :own],
        rate[:, :own],
        beta_master_ref[...],
        beta_moment_ref[...],
        beta_second_ref[...],
    )
    beta_master_out[...] = beta[0]
    beta_moment_out[...] = beta[1]
    beta_second_out[...] = beta[2]
    gain = adam_update(
        gain_ref[0:1], factor, rate, gain_ref[1:2], gain_ref[2:3], gain_ref[3:4]
    )
    stacked = jnp.concatenate(list(gain) + [jnp.zeros((TILE - 3, LANES), jnp.float32)], axis=0)
    rolled = pltpu.roll(stacked, LANES - tensor * share, 1)
    gain_master_out[...] = rolled[0:1, :share]
    gain_moment_out[...] = rolled[1:2, :share]
    gain_second_out[...] = rolled[2:3, :share]
    small = jnp.concatenate(
        [beta[0], gain[0][:, :own], jnp.zeros((TILE - heads_here - 1, own), jnp.float32)], axis=0
    )
    small = jnp.concatenate([small, small], axis=1).astype(jnp.bfloat16)
    weights_ref[own:, :LANES] = small
    weights_ref[own:, LANES:] = jnp.zeros_like(small)


def unpack_kernel(in_ref, beta_ref, gain_ref):
    heads_here = beta_ref.shape[0]
    first = lax.broadcasted_iota(jnp.int32, (TILE, LANES), 1) < LANES // 2
    for chip in range(in_ref.shape[0] // 2):
        small = jnp.where(
            first,
            in_ref[2 * chip].astype(jnp.float32),
            in_ref[2 * chip + 1].astype(jnp.float32),
        ).astype(jnp.bfloat16)
        columns = slice(chip * LANES, (chip + 1) * LANES)
        beta_ref[:, columns] = small[:heads_here]
        gain_ref[:, columns] = small[heads_here : heads_here + 1]


def per_device(
    proj_grads,
    beta_grads,
    gain_grads,
    proj_master,
    proj_moment,
    proj_second,
    beta_master,
    beta_moment,
    beta_second,
    gain_master,
    gain_moment,
    gain_second,
    learn_rate,
    clip_limit,
):
    shards = lax.axis_size("shard")
    tensor_size = lax.axis_size("tensor")
    sections = lax.axis_size("section")
    chips = shards // 2
    micro, width, columns = proj_grads.shape[2:]
    heads_here = beta_grads.shape[3]
    own = width // shards
    rows = own * (columns // LANES)
    core_pairs = [(s, s ^ 1) for s in range(shards)]
    near = []
    for side in range(2):
        for base in range(0, chips, GROUP):
            members = [(base + 2 * side + j) % chips for j in range(GROUP)]
            near.append([2 * z + side for z in sorted(members, key=lambda z: z % GROUP)])
    far = [
        [2 * (residue + high * GROUP) + side for high in range(chips // GROUP)]
        for side in range(2)
        for residue in range(GROUP)
    ]

    proj = proj_grads[0, 0].reshape(micro, chips // GROUP, 2 * GROUP, own, columns)
    beta = beta_grads[0, 0]
    gain = gain_grads[0, 0, 0]
    rate, clip = learn_rate.reshape(1), clip_limit.reshape(1)
    send, _ = pack(True, rate, clip, proj, beta, gain, rows + TILE)
    kept, scalars = pack(False, rate, clip, proj, beta, gain, rows + TILE)
    got = lax.ppermute(send, "shard", core_pairs)
    chip_sum = pl.pallas_call(
        add_kernel,
        out_shape=near_f32(kept.shape),
        in_specs=[VMEM, VMEM],
        out_specs=VMEM,
        name="core_add",
    )(kept, held(got))
    by_near = lax.all_to_all(chip_sum, "shard", 0, 0, axis_index_groups=near)
    near_sum = pl.pallas_call(
        sum_kernel, out_shape=near_f32(by_near.shape[1:]), in_specs=[VMEM], out_specs=VMEM, name="near"
    )(held(by_near))
    by_far = lax.all_to_all(near_sum, "shard", 0, 0, axis_index_groups=far)
    peers = tensor_size * sections
    total, message = pl.pallas_call(
        norm_kernel,
        out_shape=(near_f32((rows + TILE, LANES)), near_f32((peers, 1, LANES))),
        in_specs=[VMEM] * 4,
        out_specs=(VMEM, VMEM),
        name="norm",
    )(held(by_far), gain_master, gain_moment, gain_second)
    heard = lax.all_to_all(message, ("tensor", "section"), 0, 0)
    gain_rows, squares = pl.pallas_call(
        section_kernel,
        out_shape=(near_f32((TILE, LANES)), near_f32((shards, 1, LANES))),
        in_specs=[VMEM],
        out_specs=(VMEM, VMEM),
        name="section",
    )(held(heard))
    squares = lax.all_to_all(squares, "shard", 0, 0)
    counted = sections * (
        width * columns * tensor_size + heads_here * tensor_size * width + width
    )
    state = f32((own, columns))
    beta_state = f32((heads_here, own))
    gain_state = f32(gain_master.shape)
    outs = pl.pallas_call(
        functools.partial(update_kernel, counted=float(counted)),
        out_shape=(pltpu.VMEM((own + TILE, columns), jnp.bfloat16),)
        + (state,) * 3
        + (beta_state,) * 3
        + (gain_state,) * 3
        + (f32((1, LANES)),),
        in_specs=[VMEM] * 10,
        out_specs=(VMEM,) * 11,
        name="update",
    )(
        held(scalars),
        held(squares),
        held(total),
        held(gain_rows),
        proj_master[0],
        proj_moment[0],
        proj_second[0],
        beta_master[0],
        beta_moment[0],
        beta_second[0],
    )
    sent = (outs[0].astype(jnp.float32) * WIRE_SCALE).astype(WIRE)
    gathered = lax.all_gather(sent, "shard", axis=0)
    unscaled = lambda value: (value.astype(jnp.float32) * (1.0 / WIRE_SCALE)).astype(jnp.bfloat16)
    proj_weights = unscaled(gathered[:, :own])
    small = unscaled(gathered[:, own:, :LANES])
    beta_weights, gain_weights = pl.pallas_call(
        unpack_kernel,
        out_shape=(
            jax.ShapeDtypeStruct((heads_here, width), jnp.bfloat16),
            jax.ShapeDtypeStruct((1, width), jnp.bfloat16),
        ),
        in_specs=[VMEM],
        out_specs=(VMEM, VMEM),
        name="unpack",
    )(held(small))
    return (
        proj_weights.reshape(1, width, columns),
        beta_weights[None],
        gain_weights,
        outs[1][None],
        outs[2][None],
        outs[3][None],
        outs[4][None],
        outs[5][None],
        outs[6][None],
        outs[7],
        outs[8],
        outs[9],
        outs[10][0, 0],
    )


def solution(mesh):
    in_specs = (
        P("section", "shard", None, None, "tensor"),
        P("section", "shard", None, "tensor", None),
        P("section", "shard", "tensor", None, None),
        P("section", "shard", "tensor"),
        P("section", "shard", "tensor"),
        P("section", "shard", "tensor"),
        P("section", "tensor", "shard"),
        P("section", "tensor", "shard"),
        P("section", "tensor", "shard"),
        P("section", ("shard", "tensor")),
        P("section", ("shard", "tensor")),
        P("section", ("shard", "tensor")),
        P(),
        P(),
    )
    out_specs = (
        P("section", None, "tensor"),
        P("section", "tensor", None),
        P("section", None),
        P("section", "shard", "tensor"),
        P("section", "shard", "tensor"),
        P("section", "shard", "tensor"),
        P("section", "tensor", "shard"),
        P("section", "tensor", "shard"),
        P("section", "tensor", "shard"),
        P("section", ("shard", "tensor")),
        P("section", ("shard", "tensor")),
        P("section", ("shard", "tensor")),
        P(),
    )
    return jax.shard_map(
        per_device, mesh=mesh, in_specs=in_specs, out_specs=out_specs, check_vma=False
    )
```

time: 146 us -> 140 us (0.959)
  starting transfers between devices: 18.5 us -> 8.79 us
  blocking collectives: 108 us -> 116 us
  Pallas kernels: 13.6 us -> 10.8 us
  waiting for transfers between devices: 1.61 us -> 0.01 us
    ppermute x1 -> x0, starting transfers between devices: 9.68 us -> none  [per_device(): other = lax.ppermute(gathered, 'shard', core_pairs)]
    all_gather x1, blocking collectives: 22.9 us -> 31.3 us  [per_device(): gathered = lax.all_gather(sent, 'shard', axis=0)]
    pallas_call x4, Pallas kernels: 10.4 us -> 8.45 us  [the longest x2 6.09 us: pack(): pl.pallas_call(functools.partial(pack_kernel, flip=flip), in_specs=[SMEM,...]
    ppermute x1 -> x0, waiting for transfers between devices: 1.61 us -> none  [per_device(): other = lax.ppermute(gathered, 'shard', core_pairs)]
  transfers between devices with their start and end apart: 2 -> 1, of which waited for: 1 -> 0; matrix products, arithmetic and copies ran while one was open for 1% -> 0% of each run, Pallas kernels for 2% -> 2%
where the time goes in v3:
time: 140 us; the launch traced here: 139 us
  blocking collectives  116 us (83%)
  Pallas kernels  10.8 us (8%)
  starting transfers between devices  8.79 us (6%)
  between operations  2 us (1%)
    all_gather x1, blocking collectives, per_device(): gathered = lax.all_gather(sent, 'shard', axis=0)  31.3 us
    all_to_all x1, blocking collectives, per_device(): by_near = lax.all_to_all(chip_sum, 'shard', 0, 0, axis_index_groups=near)  27.9 us
    all_to_all x1, blocking collectives, per_device(): squares = lax.all_to_all(squares, 'shard', 0, 0)  25.3 us
    all_to_all x1, blocking collectives, per_device(): by_far = lax.all_to_all(near_sum, 'shard', 0, 0, axis_index_groups=far)  19 us
    all_to_all x1, blocking collectives, per_device(): heard = lax.all_to_all(message, ('tensor', 'section'), 0, 0)  13 us
    ppermute x1, starting transfers between devices, per_device(): got = lax.ppermute(send, 'shard', core_pairs)  8.79 us
    pallas_call x2, Pallas kernels, pack(): pl.pallas_call(functools.partial(pack_kernel, flip=flip), in_specs=[SMEM,...  6.09 us
  transfers between devices with their start and end apart: 1, of which 0 were waited for; matrix products, arithmetic and copies ran while one was open for 0% of the time, Pallas kernels for 2%

profile of v3, /device:TPU:1, one launch (start us, length us, event | category | flops | bytes accessed | tf_op | source)
XLA Modules:
  0.0 139.3 jit_solution(8981471821520593425)
XLA Ops:
  1.9 3.1 %pack.3 = (f32[4,4,136,128]{3,2,1,0:T(8,128)}, f32[8,128]{1,0:T(8,128)}) custom-call(f32[1]{0:T(128)} %bitcast.23.rate_ref, f32[1]{0:T(128)} %bitcast.25.clip_ref, bf16[2,4,8,64,256]{4,3,2,1,0:T(8,128)(2,1)} %bitcast.26, bf16[2,4,2048]{2,1,0:T(4,128)(2,1)} %bitcast.31, bf16[2,2048]{1,0:T(2,128)(2,1)} %bitcast.36), custom_call_target="tpu_custom_call" | custom-call | tf_op jit(solution)/shard_map/pack/pallas_call | solution.py:86
  5.0 8.8 %collective-permute-start = (f32[4,4,136,128]{3,2,1,0:T(8,128)}, f32[4,4,136,128]{3,2,1,0:T(8,128)S(1)}, u32[]{:S(2)}, u32[]{:S(2)}) collective-permute-start(f32[4,4,136,128]{3,2,1,0:T(8,128)} %get-tuple-element.35), channel_id=1, source_target_pairs={{0,16},{16,0},{32,48},{48,32},{64,80},{80,64},{96,112},{112,96},{1... | collective-permute-start | bytes 3342344 | tf_op jit(solution)/shard_map/ppermute | solution.py:309
  13.8 3.0 %pack.2 = (f32[4,4,136,128]{3,2,1,0:T(8,128)}, f32[8,128]{1,0:T(8,128)S(1)}) custom-call(f32[1]{0:T(128)} %bitcast.22.rate_ref, f32[1]{0:T(128)} %bitcast.24.clip_ref, bf16[2,4,8,64,256]{4,3,2,1,0:T(8,128)(2,1)} %bitcast.27, bf16[2,4,2048]{2,1,0:T(4,128)(2,1)} %bitcast.32, bf16[2,2048]{1,0:T(2,128)(2,1)} %bitcast.37), custom_call_target="tpu_custom_call" | custom-call | tf_op jit(solution)/shard_map/pack/pallas_call | solution.py:86
  16.8 0.0 collective-permute-done.right_ref
  16.8 1.4 core_add.1
  18.2 27.9 %all_to_all.20.in_ref = f32[4,4,136,128]{3,2,1,0:T(8,128)S(1)} all-to-all(f32[4,4,136,128]{3,2,1,0:T(8,128)S(1)} %core_add.1), channel_id=1, replica_groups={{0,32,64,96},{128,160,192,224},{256,288,320,352},{384,416,448,480},{144..., dimensions={0} | all-to-all | bytes 2228224 | tf_op jit(solution)/shard_map/all_to_all | solution.py:317
  46.1 0.1 near.1
  46.2 19.0 %all_to_all.21.in_ref = f32[4,136,128]{2,1,0:T(8,128)S(1)} all-to-all(f32[4,136,128]{2,1,0:T(8,128)S(1)} %near.1), channel_id=1, replica_groups={{0,128,256,384},{32,160,288,416},{64,192,320,448},{96,224,352,480},{16,..., dimensions={0} | all-to-all | bytes 557056 | tf_op jit(solution)/shard_map/all_to_all | solution.py:321
  65.2 0.9 norm.1
  66.0 13.0 %all_to_all.22.heard_ref = f32[16,1,128]{2,1,0:T(1,128)S(1)} all-to-all(f32[16,1,128]{2,1,0:T(1,128)S(1)} %get-tuple-element.36), channel_id=1, replica_groups=mesh['shard'=32,'tensor'=4,'section'=4] {'tensor','section'}, dimensions={0} | all-to-all | bytes 16384 | tf_op jit(solution)/shard_map/all_to_all | solution.py:330
  79.0 0.1 section.1
  79.1 25.3 %all_to_all.23.squares_ref = f32[32,1,128]{2,1,0:T(1,128)S(1)} all-to-all(f32[32,1,128]{2,1,0:T(1,128)S(1)} %get-tuple-element.37), channel_id=1, replica_groups=mesh['shard'=32,'tensor'=4,'section'=4] {'shard'}, dimensions={0} | all-to-all | bytes 32768 | tf_op jit(solution)/shard_map/all_to_all | solution.py:338
  104.4 1.7 %update.1 = (bf16[72,256]{1,0:T(8,128)(2,1)S(1)}, f32[64,256]{1,0:T(8,128)}, f32[64,256]{1,0:T(8,128)}, f32[64,256]{1,0:T(8,128)}, f32[4,64]{1,0:T(4,128)}, /*in...) custom-call(f32[8,128]{1,0:T(8,128)S(1)} %get-tuple-element.33.scala, ...), custom_call_target="tpu_custom_call" | custom-call | tf_op jit(solution)/shard_map/update/pallas_call | solution.py:345
  106.1 31.3 %all-gather.2 = f16[2304,256]{1,0:T(8,128)(2,1)S(1)} all-gather(f16[72,256]{1,0:T(8,128)(2,1)S(1)} %multiply_convert_fusion.2), channel_id=2, replica_groups=mesh['shard'=32,'tensor'=4,'section'=4] {'shard'}, dimensions={0}, use_global_device_ids=true | all-gather | bytes 1216512 | tf_op jit(solution)/shard_map/all_gather | solution.py:368
  137.4 1.2 multiply_convert_fusion
  138.7 0.6 unpack.1
  (2 shorter events, 0.0 us)
Async XLA Ops:
  5.0 11.8 %collective-permute-start = (f32[4,4,136,128]{3,2,1,0:T(8,128)}, f32[4,4,136,128]{3,2,1,0:T(8,128)S(1)}, u32[]{:S(2)}, u32[]{:S(2)}) collective-permute-start(f32[4,4,136,128]{3,2,1,0:T(8,128)} %get-tuple-element.35), channel_id=1, source_target_pairs={{0,16},{16,0},{32,48},{48,32},{64,80},{80,64},{96,112},{112,96},{1... | collective-permute-start | bytes 3342344 | tf_op jit(solution)/shard_map/ppermute | solution.py:309

commit v4 on v3

--- a/solution.py
+++ b/solution.py
@@ -16,6 +16,8 @@
 LANES = 128
 TILE = 8
 GROUP = 4
+CODE_TOP = 14.0
+CODE_STEP = 1.5 * 2.0**27
 WIRE = jnp.float16
 WIRE_SCALE = 2.0**15
 
@@ -96,6 +98,28 @@
     )(rate, clip, proj, beta, gain)
 
 
+def block_scale(rows):
+    largest = jnp.max(jnp.max(jnp.abs(rows), axis=0, keepdims=True), axis=1, keepdims=True)
+    return jnp.ceil(jnp.log2(jnp.maximum(largest, 1e-30)) + 0.01)
+
+
+def code_kernel(left_ref, right_ref, out_ref):
+    rows = left_ref.shape[2] - TILE
+    row = lax.broadcasted_iota(jnp.int32, (TILE, LANES), 0)
+    for chip in range(GROUP * GROUP):
+        place = (chip % GROUP, chip // GROUP)
+        proj = left_ref[place + (slice(0, rows),)] + right_ref[place + (slice(0, rows),)]
+        tail = left_ref[place + (slice(rows, None),)] + right_ref[place + (slice(rows, None),)]
+        proj_scale, tail_scale = block_scale(proj), block_scale(tail)
+        out_ref[chip, :rows, :] = proj * jnp.exp2(CODE_TOP - proj_scale)
+        tail = tail * jnp.exp2(CODE_TOP - tail_scale)
+        high = (tail + CODE_STEP) - CODE_STEP
+        low = tail - high
+        high = jnp.where(row == TILE - 2, proj_scale, jnp.where(row == TILE - 1, tail_scale, high))
+        out_ref[chip, rows : rows + TILE, :] = high
+        out_ref[chip, rows + TILE :, :] = low
+
+
 def add_kernel(left_ref, right_ref, out_ref):
     out_ref[...] = left_ref[...] + right_ref[...]
 
@@ -104,24 +128,19 @@
     out_ref[...] = (in_ref[0] + in_ref[1]) + (in_ref[2] + in_ref[3])
 
 
-def norm_kernel(in_ref, master_ref, moment_ref, second_ref, total_ref, message_ref):
+def norm_message(total, failed, master_ref, moment_ref, second_ref, total_ref, message_ref):
     rows = total_ref.shape[0] - TILE
     own = LANES // 2
     heads_here = TILE // 2
     share = master_ref.shape[1]
     core = lax.axis_index("shard") % 2
-    total = (in_ref[0] + in_ref[1]) + (in_ref[2] + in_ref[3])
     tail = pltpu.roll(total[rows:], LANES - core * own, 1)
     total_ref[:rows, :] = total[:rows]
     total_ref[rows:, :] = tail
-    squares = total[:rows] * total[:rows]
-    folded = squares[0:TILE]
-    for row in range(TILE, rows, TILE):
-        folded = folded + squares[row : row + TILE]
+    folded = fold(total[:rows] * total[:rows])
     lane = lax.broadcasted_iota(jnp.int32, (TILE, LANES), 1)
     row = lax.broadcasted_iota(jnp.int32, (TILE, LANES), 0)
-    folded = folded + jnp.where((lane < own) & (row < heads_here), tail * tail, 0.0)
-    local = jnp.sum(jnp.sum(folded, axis=0, keepdims=True), axis=1, keepdims=True)
+    local = whole(folded + jnp.where((lane < own) & (row < heads_here), tail * tail, 0.0))
     state = jnp.concatenate(
         [
             jnp.zeros((1, LANES - 3 * share), jnp.float32),
@@ -132,13 +151,53 @@
         axis=1,
     )
     lane = lane[0:1]
-    message = jnp.where(
-        lane < own,
-        tail[heads_here : heads_here + 1],
-        jnp.where(lane == own, local, state),
-    )
+    message = jnp.where(lane < own, tail[heads_here : heads_here + 1], state)
+    message = jnp.where(lane == own, local, message)
+    message = jnp.where(lane == own + 1, failed, message)
     for peer in range(message_ref.shape[0]):
         message_ref[peer] = message
+
+
+def fold(rows):
+    folded = rows[0:TILE]
+    for row in range(TILE, rows.shape[0], TILE):
+        folded = folded + rows[row : row + TILE]
+    return folded
+
+
+def whole(tile):
+    return jnp.sum(jnp.sum(tile, axis=0, keepdims=True), axis=1, keepdims=True)
+
+
+def exact_norm_kernel(in_ref, *refs):
+    total = (in_ref[0] + in_ref[1]) + (in_ref[2] + in_ref[3])
+    norm_message(total, jnp.zeros((1, 1), jnp.float32), *refs)
+
+
+def coded_norm_kernel(in_ref, *refs):
+    rows = in_ref.shape[1] - 2 * TILE
+    proj = jnp.zeros((rows, LANES), jnp.float32)
+    power = jnp.zeros((rows, LANES), jnp.float32)
+    tail = jnp.zeros((TILE, LANES), jnp.float32)
+    for chip in range(in_ref.shape[0]):
+        high = in_ref[chip, rows : rows + TILE, :]
+        part = in_ref[chip, :rows, :] * jnp.exp2(high[TILE - 2 : TILE - 1] - CODE_TOP)
+        proj = proj + part
+        power = power + part * part
+        tail = tail + (high + in_ref[chip, rows + TILE :, :]) * jnp.exp2(
+            high[TILE - 1 : TILE] - CODE_TOP
+        )
+    squares = proj * proj
+    largest = jnp.max(jnp.max(squares, axis=0, keepdims=True), axis=1, keepdims=True)
+    inverse = jnp.where(largest > 0.0, 1.0 / jnp.maximum(largest, 1e-37), 0.0)
+    share = squares * inverse
+    spread = power * inverse
+    passed = (whole(fold(spread)) <= 1.5 * whole(fold(share))) & (
+        whole(fold(share * spread)) <= whole(fold(share * share))
+    )
+    passed = passed & ((largest > 0.0) | (whole(fold(power)) <= 0.0))
+    total = jnp.concatenate([proj, tail], axis=0)
+    norm_message(total, jnp.where(passed, 0.0, 1.0), *refs)
 
 
 def section_kernel(heard_ref, gain_ref, message_ref):
@@ -154,7 +213,7 @@
         rows = [heard_ref[rank * sections + other] for rank in range(GROUP)]
         summed = (rows[0] + rows[1]) + (rows[2] + rows[3])
         counted = counted + jnp.where(
-            lane < own, summed * summed, jnp.where(lane == own, summed, 0.0)
+            lane < own, summed * summed, jnp.where(lane <= own + 1, summed, 0.0)
         )
         here = here + jnp.where(section == other, summed, 0.0)
         ranks = [
@@ -169,7 +228,9 @@
             state = jnp.where(lane // share == rank, moved, state)
         gain_ref[kind + 1 : kind + 2, :] = state
     gain_ref[4:, :] = jnp.zeros((TILE - 4, LANES), jnp.float32)
-    total = jnp.broadcast_to(jnp.sum(counted, axis=1, keepdims=True), (1, LANES))
+    failed = jnp.sum(jnp.where(lane == own + 1, counted, 0.0), axis=1, keepdims=True)
+    total = jnp.sum(jnp.where(lane == own + 1, 0.0, counted), axis=1, keepdims=True)
+    total = jnp.where(lane == LANES - 1, failed, total)
     for peer in range(message_ref.shape[0]):
         message_ref[peer] = total
 
@@ -206,6 +267,7 @@
     rows = total_ref.shape[0] - TILE
     rate = scalars_ref[0:1, :]
     squares = jnp.sum(squares_ref[...], axis=0)
+    squares = jnp.broadcast_to(squares[:, 0:1], squares.shape)
     rms_ref[...] = jnp.sqrt(squares / counted)
     factor = jnp.minimum(1.0, scalars_ref[1:2, :] / (jnp.sqrt(squares) + norm_eps))
     for half in range(rows // own):
@@ -304,38 +366,66 @@
     beta = beta_grads[0, 0]
     gain = gain_grads[0, 0, 0]
     rate, clip = learn_rate.reshape(1), clip_limit.reshape(1)
-    send, _ = pack(True, rate, clip, proj, beta, gain, rows + TILE)
-    kept, scalars = pack(False, rate, clip, proj, beta, gain, rows + TILE)
-    got = lax.ppermute(send, "shard", core_pairs)
-    chip_sum = pl.pallas_call(
-        add_kernel,
-        out_shape=near_f32(kept.shape),
+    states = (gain_master, gain_moment, gain_second)
+    peers = tensor_size * sections
+
+    def chip_parts():
+        send, _ = pack(True, rate, clip, proj, beta, gain, rows + TILE)
+        kept, scalars = pack(False, rate, clip, proj, beta, gain, rows + TILE)
+        got = lax.ppermute(send, "shard", core_pairs)
+        return kept, got, scalars
+
+    def totals(kernel, value):
+        total, message = pl.pallas_call(
+            kernel,
+            out_shape=(near_f32((rows + TILE, LANES)), near_f32((peers, 1, LANES))),
+            in_specs=[VMEM] * 4,
+            out_specs=(VMEM, VMEM),
+            name="norm",
+        )(held(value), *states)
+        heard = lax.all_to_all(message, ("tensor", "section"), 0, 0)
+        gain_rows, squares = pl.pallas_call(
+            section_kernel,
+            out_shape=(near_f32((TILE, LANES)), near_f32((shards, 1, LANES))),
+            in_specs=[VMEM],
+            out_specs=(VMEM, VMEM),
+            name="section",
+        )(held(heard))
+        return total, gain_rows, lax.all_to_all(squares, "shard", 0, 0)
+
+    def exact_totals(*_):
+        kept, got, _ = chip_parts()
+        chip_sum = pl.pallas_call(
+            add_kernel,
+            out_shape=near_f32(kept.shape),
+            in_specs=[VMEM, VMEM],
+            out_specs=VMEM,
+            name="core_add",
+        )(kept, held(got))
+        by_near = lax.all_to_all(chip_sum, "shard", 0, 0, axis_index_groups=near)
+        near_sum = pl.pallas_call(
+            sum_kernel,
+            out_shape=near_f32(by_near.shape[1:]),
+            in_specs=[VMEM],
+            out_specs=VMEM,
+            name="near",
+        )(held(by_near))
+        by_far = lax.all_to_all(near_sum, "shard", 0, 0, axis_index_groups=far)
+        return totals(exact_norm_kernel, by_far)
+
+    kept, got, scalars = chip_parts()
+    coded = pl.pallas_call(
+        code_kernel,
+        out_shape=near_f32((chips, rows + 2 * TILE, LANES)),
         in_specs=[VMEM, VMEM],
         out_specs=VMEM,
-        name="core_add",
+        name="code",
     )(kept, held(got))
-    by_near = lax.all_to_all(chip_sum, "shard", 0, 0, axis_index_groups=near)
-    near_sum = pl.pallas_call(
-        sum_kernel, out_shape=near_f32(by_near.shape[1:]), in_specs=[VMEM], out_specs=VMEM, name="near"
-    )(held(by_near))
-    by_far = lax.all_to_all(near_sum, "shard", 0, 0, axis_index_groups=far)
-    peers = tensor_size * sections
-    total, message = pl.pallas_call(
-        norm_kernel,
-        out_shape=(near_f32((rows + TILE, LANES)), near_f32((peers, 1, LANES))),
-        in_specs=[VMEM] * 4,
-        out_specs=(VMEM, VMEM),
-        name="norm",
-    )(held(by_far), gain_master, gain_moment, gain_second)
-    heard = lax.all_to_all(message, ("tensor", "section"), 0, 0)
-    gain_rows, squares = pl.pallas_call(
-        section_kernel,
-        out_shape=(near_f32((TILE, LANES)), near_f32((shards, 1, LANES))),
-        in_specs=[VMEM],
-        out_specs=(VMEM, VMEM),
-        name="section",
-    )(held(heard))
-    squares = lax.all_to_all(squares, "shard", 0, 0)
+    z_groups = [[2 * z + side for z in range(chips)] for side in range(2)]
+    by_chip = lax.all_to_all(coded.astype(WIRE), "shard", 0, 0, axis_index_groups=z_groups)
+    quick = totals(coded_norm_kernel, by_chip.astype(jnp.float32))
+    failed = jnp.sum(quick[2][:, 0, LANES - 1]) > 0.0
+    total, gain_rows, squares = lax.cond(failed, exact_totals, lambda *given: given, *quick)
     counted = sections * (
         width * columns * tensor_size + heads_here * tensor_size * width + width
     )
@@ -357,12 +447,12 @@
         held(squares),
         held(total),
         held(gain_rows),
-        proj_master[0],
-        proj_moment[0],
-        proj_second[0],
-        beta_master[0],
-        beta_moment[0],
-        beta_second[0],
+        held(proj_master[0]),
+        held(proj_moment[0]),
+        held(proj_second[0]),
+        held(beta_master[0]),
+        held(beta_moment[0]),
+        held(beta_second[0]),
     )
     sent = (outs[0].astype(jnp.float32) * WIRE_SCALE).astype(WIRE)
     gathered = lax.all_gather(sent, "shard", axis=0)

time: 140 us -> 133 us (0.950)
  blocking collectives: 116 us -> 87.4 us
  waiting for transfers between devices: 0.01 us -> 13.1 us
  starting transfers between devices: 8.79 us -> 15.9 us
  local copies, waits for them, and re-layouts: 0 us -> 2.51 us
  Pallas kernels: 10.8 us -> 8.36 us
    all_to_all x4 -> x2, blocking collectives: 85.2 us -> 56.2 us  [the longest x1 43.1 us: per_device(): lax.all_to_all(coded.astype(WIRE), 'shard', 0, 0, axis_index_groups=z_gro...]
    all_to_all x0 -> x1, waiting for transfers between devices: none -> 11.8 us  [totals(): return (total, gain_rows, lax.all_to_all(squares, 'shard', 0, 0))]
    all_to_all x0 -> x1, starting transfers between devices: none -> 7.13 us  [totals(): return (total, gain_rows, lax.all_to_all(squares, 'shard', 0, 0))]
    unnamed x0 -> x26, local copies, waits for them, and re-layouts: none -> 2.51 us
    pallas_call x2, Pallas kernels: 6.09 us -> 4.28 us  [pack(): pl.pallas_call(functools.partial(pack_kernel, flip=flip), in_specs=[SMEM,...]
  transfers between devices with their start and end apart: 1 -> 2, of which waited for: 0 -> 2; matrix products, arithmetic and copies ran while one was open for 0% -> 0% of each run, Pallas kernels for 2% -> 1%
where the time goes in v4:
time: 133 us; the launch traced here: 132 us
  blocking collectives  87.4 us (66%)
  starting transfers between devices  15.9 us (12%)
  waiting for transfers between devices  13.1 us (10%)
  Pallas kernels  8.36 us (6%)
  between operations  2.96 us (2%)
  local copies, waits for them, and re-layouts  2.51 us (2%)
  other arithmetic  2.14 us (2%)
    all_to_all x1, blocking collectives, per_device(): lax.all_to_all(coded.astype(WIRE), 'shard', 0, 0, axis_index_groups=z_gro...  43.1 us
    all_gather x1, blocking collectives, per_device(): gathered = lax.all_gather(sent, 'shard', axis=0)  31.3 us
    all_to_all x1, blocking collectives, totals(): heard = lax.all_to_all(message, ('tensor', 'section'), 0, 0)  13.1 us
    all_to_all x1, waiting for transfers between devices, totals(): return (total, gain_rows, lax.all_to_all(squares, 'shard', 0, 0))  11.8 us
    ppermute x1, starting transfers between devices, chip_parts(): got = lax.ppermute(send, 'shard', core_pairs)  8.79 us
    all_to_all x1, starting transfers between devices, totals(): return (total, gain_rows, lax.all_to_all(squares, 'shard', 0, 0))  7.13 us
    pallas_call x2, Pallas kernels, pack(): pl.pallas_call(functools.partial(pack_kernel, flip=flip), in_specs=[SMEM,...  4.28 us
  transfers between devices with their start and end apart: 2, of which 2 were waited for; matrix products, arithmetic and copies ran while one was open for 0% of the time, Pallas kernels for 1%

profile of v4, /device:TPU:1, one launch (start us, length us, event | category | flops | bytes accessed | tf_op | source)
XLA Modules:
  0.0 132.4 jit_solution(3455530630613175927)
XLA Ops:
  0.6 0.0 copy-start.6
  0.7 0.0 copy-start.8
  0.7 0.0 copy-start.9
  2.1 3.0 %pack.7 = (f32[4,4,136,128]{3,2,1,0:T(8,128)}, f32[8,128]{1,0:T(8,128)}) custom-call(f32[1]{0:T(128)} %bitcast.23.rate_ref, f32[1]{0:T(128)} %bitcast.25.clip_ref, bf16[2,4,8,64,256]{4,3,2,1,0:T(8,128)(2,1)} %bitcast.32, bf16[2,4,2048]{2,1,0:T(4,128)(2,1)} %bitcast.38, bf16[2,2048]{1,0:T(2,128)(2,1)} %bitcast.41), custom_call_target="tpu_custom_call" | custom-call | tf_op jit(solution)/shard_map/pack/pallas_call | solution.py:88
  5.1 8.8 %collective-permute-start.1 = (f32[4,4,136,128]{3,2,1,0:T(8,128)}, f32[4,4,136,128]{3,2,1,0:T(8,128)S(1)}, u32[]{:S(2)}, u32[]{:S(2)}) collective-permute-start(f32[4,4,136,128]{3,2,1,0:T(8,128)} %get-tuple-element.74), channel_id=1, source_target_pairs={{0,16},{16,0},{32,48},{48,32},{64,80},{80,64},{96,112},{112,96},{1... | collective-permute-start | bytes 3342344 | tf_op jit(solution)/shard_map/ppermute | solution.py:375
  13.9 0.0 copy-done.6
  13.9 0.0 copy-done.8
  13.9 0.0 copy-done.9
  14.0 1.3 pack.6
  15.2 1.3 collective-permute-done.1.right_ref
  16.5 1.6 %code.1 = f32[16,144,128]{2,1,0:T(8,128)S(1)} custom-call(f32[4,4,136,128]{3,2,1,0:T(8,128)} %get-tuple-element.73.left_ref, f32[4,4,136,128]{3,2,1,0:T(8,128)S(1)} %collective-permute-done.1.right_ref), custom_call_target="tpu_custom_call" | custom-call | tf_op jit(solution)/shard_map/code/pallas_call | solution.py:417
  18.1 0.1 convert_element_type.27
  18.2 0.0 copy-start.10
  18.2 0.0 copy-start.11
  18.2 0.0 copy-start.12
  18.2 43.1 %all_to_all.35 = f16[16,144,128]{2,1,0:T(8,128)(2,1)S(1)} all-to-all(f16[16,144,128]{2,1,0:T(8,128)(2,1)S(1)} %convert_element_type.27), channel_id=1, replica_groups={{0,32,64,96,128,160,192,224,256,288,320,352,384,416,448,480},{16,48,80,..., dimensions={0} | all-to-all | bytes 1179648 | tf_op jit(solution)/shard_map/all_to_all | solution.py:425
  61.3 0.0 copy-start.7
  61.3 0.1 convert_element_type.28.in_ref
  61.3 0.0 copy-done.10
  61.4 0.0 copy-done.11
  61.4 0.0 copy-done.12
  61.4 0.4 norm.3
  61.7 13.1 %all_to_all.36.heard_ref = f32[16,1,128]{2,1,0:T(1,128)S(1)} all-to-all(f32[16,1,128]{2,1,0:T(1,128)S(1)} %get-tuple-element.75), channel_id=1, replica_groups=mesh['shard'=32,'tensor'=4,'section'=4] {'tensor','section'}, dimensions={0} | all-to-all | bytes 16384 | tf_op jit(solution)/shard_map/all_to_all | solution.py:386
  74.8 0.7 section.3
  75.5 7.1 %all-to-all-start.6 = ((f32[32,1,128]{2,1,0:T(1,128)}), f32[32,1,128]{2,1,0:T(1,128)S(1)}, u32[]{:S(2)}, u32[]{:S(2)}) async-start(f32[32,1,128]{2,1,0:T(1,128)} %get-tuple-element.76), calls=%async_computation.6 | async-start | bytes 32768 | tf_op jit(solution)/shard_map/all_to_all | solution.py:394
  82.7 11.8 %all-to-all-done.6 = f32[32,1,128]{2,1,0:T(1,128)S(1)} async-done(((f32[32,1,128]{2,1,0:T(1,128)}), f32[32,1,128]{2,1,0:T(1,128)S(1)}, u32[]{:S(2)}, u32[]{:S(2)}) %all-to-all-start.6) | async-done | bytes 16416 | tf_op jit(solution)/shard_map/all_to_all | solution.py:394
  94.5 0.7 slice_reduce_fusion
  95.8 0.0 copy-done.7
  95.8 0.0 copy-start
  95.9 0.0 copy-start.3
  95.9 0.0 copy-start.4
  95.9 0.0 copy-start.5
  95.9 0.8 copy-done
  96.7 0.0 copy-done.3
  96.7 0.0 copy-done.4
  96.7 0.0 copy-done.5
  96.7 0.0 copy-start.1
  96.7 0.8 copy-done.1
  97.5 0.0 copy-start.2
  97.5 0.8 copy-done.2
  98.4 0.8 update.1
  99.2 31.3 %all-gather.2 = f16[2304,256]{1,0:T(8,128)(2,1)S(1)} all-gather(f16[72,256]{1,0:T(8,128)(2,1)S(1)} %multiply_convert_fusion.2), channel_id=2, replica_groups=mesh['shard'=32,'tensor'=4,'section'=4] {'shard'}, dimensions={0}, use_global_device_ids=true | all-gather | bytes 1216512 | tf_op jit(solution)/shard_map/all_gather | solution.py:458
  130.5 1.3 multiply_convert_fusion
  131.8 0.6 unpack.1
  (3 shorter events, 0.0 us)
Async XLA Ops:
  0.6 13.3 %copy-start.6 = (bf16[1,1,2,2048,256]{4,3,2,1,0:T(8,128)(2,1)S(1)}, bf16[1,1,2,2048,256]{4,3,2,1,0:T(8,128)(2,1)}, u32[]{:S(2)}) copy-start(bf16[1,1,2,2048,256]{4,3,2,1,0:T(8,128)(2,1)} %param.16) | copy-start | bytes 6291460
  0.7 13.3 %copy-start.8 = (bf16[1,1,2,4,2048]{4,3,2,1,0:T(4,128)(2,1)S(1)}, bf16[1,1,2,4,2048]{4,3,2,1,0:T(4,128)(2,1)}, u32[]{:S(2)}) copy-start(bf16[1,1,2,4,2048]{4,3,2,1,0:T(4,128)(2,1)} %param.17) | copy-start | bytes 98308
  0.7 13.3 %copy-start.9 = (bf16[1,1,1,2,2048]{4,3,2,1,0:T(2,128)(2,1)S(1)}, bf16[1,1,1,2,2048]{4,3,2,1,0:T(2,128)(2,1)}, u32[]{:S(2)}) copy-start(bf16[1,1,1,2,2048]{4,3,2,1,0:T(2,128)(2,1)} %param.18) | copy-start | bytes 24580
  5.1 11.4 %collective-permute-start.1 = (f32[4,4,136,128]{3,2,1,0:T(8,128)}, f32[4,4,136,128]{3,2,1,0:T(8,128)S(1)}, u32[]{:S(2)}, u32[]{:S(2)}) collective-permute-start(f32[4,4,136,128]{3,2,1,0:T(8,128)} %get-tuple-element.74), channel_id=1, source_target_pairs={{0,16},{16,0},{32,48},{48,32},{64,80},{80,64},{96,112},{112,96},{1... | collective-permute-start | bytes 3342344 | tf_op jit(solution)/shard_map/ppermute | solution.py:375
  18.2 43.2 %copy-start.10 = (f32[1,16]{1,0:T(1,128)S(1)}, f32[1,16]{1,0:T(1,128)}, u32[]{:S(2)}) copy-start(f32[1,16]{1,0:T(1,128)} %refs_0_.1) | copy-start | bytes 196
  18.2 43.2 %copy-start.11 = (f32[1,16]{1,0:T(1,128)S(1)}, f32[1,16]{1,0:T(1,128)}, u32[]{:S(2)}) copy-start(f32[1,16]{1,0:T(1,128)} %refs_1_.1) | copy-start | bytes 196
  18.2 43.2 %copy-start.12 = (f32[1,16]{1,0:T(1,128)S(1)}, f32[1,16]{1,0:T(1,128)}, u32[]{:S(2)}) copy-start(f32[1,16]{1,0:T(1,128)} %refs_2_.1) | copy-start | bytes 196
  61.3 34.6 %copy-start.7 = (bf16[1,1,2,2048,256]{4,3,2,1,0:T(8,128)(2,1)S(1)}, bf16[1,1,2,2048,256]{4,3,2,1,0:T(8,128)(2,1)}, u32[]{:S(2)}) copy-start(bf16[1,1,2,2048,256]{4,3,2,1,0:T(8,128)(2,1)} %param.16) | copy-start | bytes 6291460
  75.5 18.9 %all-to-all-start.6 = ((f32[32,1,128]{2,1,0:T(1,128)}), f32[32,1,128]{2,1,0:T(1,128)S(1)}, u32[]{:S(2)}, u32[]{:S(2)}) async-start(f32[32,1,128]{2,1,0:T(1,128)} %get-tuple-element.76), calls=%async_computation.6 | async-start | bytes 32768 | tf_op jit(solution)/shard_map/all_to_all | solution.py:394
  95.8 0.8 copy-start
  95.9 0.8 copy-start.3
  95.9 0.8 copy-start.4
  95.9 0.8 copy-start.5
  96.7 0.8 copy-start.1
  97.5 0.8 copy-start.2

commit v5 on v4

--- a/solution.py
+++ b/solution.py
@@ -21,6 +21,7 @@
 WIRE = jnp.float16
 WIRE_SCALE = 2.0**15
 
+SMALL = pltpu.CompilerParams(vmem_limit_bytes=8 * 2**20)
 VMEM = pl.BlockSpec(memory_space=pltpu.VMEM)
 SMEM = pl.BlockSpec(memory_space=pltpu.SMEM)
 
@@ -47,55 +48,88 @@
     return pltpu.with_memory_space_constraint(value, pltpu.VMEM)
 
 
-def pack_kernel(rate_ref, clip_ref, proj_ref, beta_ref, gain_ref, out_ref, scalars_ref, buffer, arrived, *, flip):
-    heads_here = beta_ref.shape[1]
-    own = proj_ref.shape[3]
-    core = lax.axis_index("shard") % 2
-    which = 1 - core if flip else core
-    copies = [
-        pltpu.make_async_copy(
-            proj_ref.at[:, :, 2 * residue + which], buffer.at[residue], arrived.at[residue]
-        )
-        for residue in range(GROUP)
-    ]
-    for copy in copies:
-        copy.start()
-    lane = lax.broadcasted_iota(jnp.int32, scalars_ref.shape, 0)
-    scalars_ref[...] = jnp.where(lane == 0, rate_ref[0], clip_ref[0])
+def tail_rows(beta_ref, gain_ref):
     beta = beta_ref[0].astype(jnp.float32) + beta_ref[1].astype(jnp.float32)
     gain = gain_ref[...].astype(jnp.float32)
-    gain = gain[0:1] + gain[1:2]
-    blank = jnp.zeros((TILE - heads_here - 1, LANES), jnp.float32)
-    for chip in range(GROUP * GROUP):
-        columns = slice(chip * LANES, (chip + 1) * LANES)
-        out_ref[chip % GROUP, chip // GROUP, 2 * own :, :] = jnp.concatenate(
-            [beta[:, columns], gain[:, columns], blank], axis=0
+    blank = jnp.zeros((TILE - beta.shape[0] - 1, beta.shape[1]), jnp.float32)
+    return jnp.concatenate([beta, gain[0:1] + gain[1:2], blank], axis=0)
+
+
+def stack_halves(rows):
+    return jnp.concatenate(
+        [rows[:, start : start + LANES] for start in range(0, rows.shape[1], LANES)], axis=0
+    )
+
+
+def proj_rows(proj_ref, chip, core):
+    place = (chip // GROUP, chip % GROUP, core)
+    return stack_halves(
+        proj_ref[(0,) + place].astype(jnp.float32) + proj_ref[(1,) + place].astype(jnp.float32)
+    )
+
+
+def pack_kernel(
+    proj_ref,
+    beta_ref,
+    gain_ref,
+    gain_master_ref,
+    gain_moment_ref,
+    gain_second_ref,
+    out_ref,
+    tails_ref,
+    state_ref,
+    buffer,
+    staged,
+    arrived,
+    sent,
+):
+    other = 1 - lax.axis_index("shard") % 2
+    arrivals = [
+        pltpu.make_async_copy(
+            proj_ref.at[:, high, :, other], buffer.at[high], arrived.at[high]
         )
-    for residue in range(GROUP):
-        copies[residue].wait()
-        for high in range(GROUP):
-            rows = buffer[residue, 0, high].astype(jnp.float32) + buffer[residue, 1, high].astype(
-                jnp.float32
+        for high in range(GROUP)
+    ]
+    for copy in arrivals:
+        copy.start()
+    tails = tail_rows(beta_ref, gain_ref)
+    tails_ref[...] = tails
+    state = gain_state_row(gain_master_ref, gain_moment_ref, gain_second_ref)
+    state_ref[...] = jnp.broadcast_to(state, state_ref.shape)
+    rows = staged.shape[1] - TILE
+    departures = []
+    for high in range(GROUP):
+        arrivals[high].wait()
+        for low in range(GROUP):
+            chip = high * GROUP + low
+            staged[chip, :rows, :] = stack_halves(
+                buffer[high, 0, low].astype(jnp.float32) + buffer[high, 1, low].astype(jnp.float32)
             )
-            for half in range(rows.shape[1] // LANES):
-                out_ref[residue, high, half * own : (half + 1) * own, :] = rows[
-                    :, half * LANES : (half + 1) * LANES
-                ]
-
-
-def pack(flip, rate, clip, proj, beta, gain, rows):
-    own, columns = proj.shape[3:]
+            staged[chip, rows:, :] = tails[:, chip * LANES : (chip + 1) * LANES]
+        part = pl.ds(high * GROUP, GROUP)
+        departures.append(pltpu.make_async_copy(staged.at[part], out_ref.at[part], sent.at[high]))
+        departures[-1].start()
+    for copy in departures:
+        copy.wait()
+
+
+def pack(proj, beta, gain, states, rows):
+    own, columns = proj.shape[4:]
+    shape = (GROUP * GROUP, rows, LANES)
     return pl.pallas_call(
-        functools.partial(pack_kernel, flip=flip),
-        in_specs=[SMEM, SMEM, pl.BlockSpec(memory_space=pl.ANY), VMEM, VMEM],
-        out_specs=(VMEM, VMEM),
-        out_shape=(f32((GROUP, GROUP, rows, LANES)), near_f32((TILE, LANES))),
+        pack_kernel,
+        in_specs=[pl.BlockSpec(memory_space=pl.ANY)] + [VMEM] * 5,
+        out_specs=(pl.BlockSpec(memory_space=pl.ANY), VMEM, VMEM),
+        out_shape=(f32(shape), near_f32((TILE, gain.shape[1])), near_f32((TILE, LANES))),
         scratch_shapes=[
             pltpu.VMEM((GROUP, 2, GROUP, own, columns), jnp.bfloat16),
+            pltpu.VMEM(shape, jnp.float32),
+            pltpu.SemaphoreType.DMA((GROUP,)),
             pltpu.SemaphoreType.DMA((GROUP,)),
         ],
         name="pack",
-    )(rate, clip, proj, beta, gain)
+        compiler_params=SMALL,
+    )(proj, beta, gain, *states)
 
 
 def block_scale(rows):
@@ -103,53 +137,57 @@
     return jnp.ceil(jnp.log2(jnp.maximum(largest, 1e-30)) + 0.01)
 
 
-def code_kernel(left_ref, right_ref, out_ref):
-    rows = left_ref.shape[2] - TILE
+def gain_state_row(*refs):
+    states = [ref[...] for ref in refs]
+    share = states[0].shape[1]
+    return jnp.concatenate([jnp.zeros((1, LANES - 3 * share), jnp.float32)] + states, axis=1)
+
+
+def code_kernel(rate_ref, clip_ref, proj_ref, tails_ref, got_ref, out_ref, scalars_ref):
     row = lax.broadcasted_iota(jnp.int32, (TILE, LANES), 0)
+    scalars_ref[...] = jnp.where(row == 0, rate_ref[0], clip_ref[0])
+    rows = got_ref.shape[1] - TILE
+    own = LANES // 2
+    core = lax.axis_index("shard") % 2
+    left_half = lax.broadcasted_iota(jnp.int32, (TILE, LANES), 1) < own
     for chip in range(GROUP * GROUP):
-        place = (chip % GROUP, chip // GROUP)
-        proj = left_ref[place + (slice(0, rows),)] + right_ref[place + (slice(0, rows),)]
-        tail = left_ref[place + (slice(rows, None),)] + right_ref[place + (slice(rows, None),)]
+        proj = proj_rows(proj_ref, chip, core) + got_ref[chip, :rows, :]
+        tail = tails_ref[:, chip * LANES : (chip + 1) * LANES] + got_ref[chip, rows:, :]
+        tail = pltpu.roll(tail, LANES - core * own, 1)
         proj_scale, tail_scale = block_scale(proj), block_scale(tail)
         out_ref[chip, :rows, :] = proj * jnp.exp2(CODE_TOP - proj_scale)
         tail = tail * jnp.exp2(CODE_TOP - tail_scale)
         high = (tail + CODE_STEP) - CODE_STEP
-        low = tail - high
-        high = jnp.where(row == TILE - 2, proj_scale, jnp.where(row == TILE - 1, tail_scale, high))
-        out_ref[chip, rows : rows + TILE, :] = high
-        out_ref[chip, rows + TILE :, :] = low
-
-
-def add_kernel(left_ref, right_ref, out_ref):
-    out_ref[...] = left_ref[...] + right_ref[...]
+        low = pltpu.roll(tail - high, own, 1)
+        tail = jnp.where(left_half, high, low)
+        tail = jnp.where(row == TILE - 2, proj_scale, jnp.where(row == TILE - 1, tail_scale, tail))
+        out_ref[chip, rows:, :] = tail
+
+
+def add_kernel(proj_ref, tails_ref, got_ref, out_ref):
+    rows = got_ref.shape[1] - TILE
+    core = lax.axis_index("shard") % 2
+    for chip in range(GROUP * GROUP):
+        place = (chip % GROUP, chip // GROUP)
+        tail = tails_ref[:, chip * LANES : (chip + 1) * LANES]
+        out_ref[place + (slice(0, rows),)] = proj_rows(proj_ref, chip, core) + got_ref[chip, :rows, :]
+        out_ref[place + (slice(rows, None),)] = tail + got_ref[chip, rows:, :]
 
 
 def sum_kernel(in_ref, out_ref):
     out_ref[...] = (in_ref[0] + in_ref[1]) + (in_ref[2] + in_ref[3])
 
 
-def norm_message(total, failed, master_ref, moment_ref, second_ref, total_ref, message_ref):
+def norm_message(total, failed, state, total_ref, message_ref):
     rows = total_ref.shape[0] - TILE
     own = LANES // 2
     heads_here = TILE // 2
-    share = master_ref.shape[1]
-    core = lax.axis_index("shard") % 2
-    tail = pltpu.roll(total[rows:], LANES - core * own, 1)
-    total_ref[:rows, :] = total[:rows]
-    total_ref[rows:, :] = tail
+    tail = total[rows:]
+    total_ref[...] = total
     folded = fold(total[:rows] * total[:rows])
     lane = lax.broadcasted_iota(jnp.int32, (TILE, LANES), 1)
     row = lax.broadcasted_iota(jnp.int32, (TILE, LANES), 0)
     local = whole(folded + jnp.where((lane < own) & (row < heads_here), tail * tail, 0.0))
-    state = jnp.concatenate(
-        [
-            jnp.zeros((1, LANES - 3 * share), jnp.float32),
-            master_ref[...],
-            moment_ref[...],
-            second_ref[...],
-        ],
-        axis=1,
-    )
     lane = lane[0:1]
     message = jnp.where(lane < own, tail[heads_here : heads_here + 1], state)
     message = jnp.where(lane == own, local, message)
@@ -169,23 +207,27 @@
     return jnp.sum(jnp.sum(tile, axis=0, keepdims=True), axis=1, keepdims=True)
 
 
-def exact_norm_kernel(in_ref, *refs):
+def exact_norm_kernel(in_ref, state_ref, *refs):
     total = (in_ref[0] + in_ref[1]) + (in_ref[2] + in_ref[3])
-    norm_message(total, jnp.zeros((1, 1), jnp.float32), *refs)
-
-
-def coded_norm_kernel(in_ref, *refs):
-    rows = in_ref.shape[1] - 2 * TILE
+    rows = total.shape[0] - TILE
+    shift = LANES - lax.axis_index("shard") % 2 * (LANES // 2)
+    total = jnp.concatenate([total[:rows], pltpu.roll(total[rows:], shift, 1)], axis=0)
+    norm_message(total, jnp.zeros((1, 1), jnp.float32), state_ref[0:1, :], *refs)
+
+
+def coded_norm_kernel(in_ref, state_ref, *refs):
+    rows = in_ref.shape[1] - TILE
+    own = LANES // 2
     proj = jnp.zeros((rows, LANES), jnp.float32)
     power = jnp.zeros((rows, LANES), jnp.float32)
     tail = jnp.zeros((TILE, LANES), jnp.float32)
     for chip in range(in_ref.shape[0]):
-        high = in_ref[chip, rows : rows + TILE, :]
-        part = in_ref[chip, :rows, :] * jnp.exp2(high[TILE - 2 : TILE - 1] - CODE_TOP)
+        coded = in_ref[chip, rows:, :]
+        part = in_ref[chip, :rows, :] * jnp.exp2(coded[TILE - 2 : TILE - 1] - CODE_TOP)
         proj = proj + part
         power = power + part * part
-        tail = tail + (high + in_ref[chip, rows + TILE :, :]) * jnp.exp2(
-            high[TILE - 1 : TILE] - CODE_TOP
+        tail = tail + (coded + pltpu.roll(coded, own, 1)) * jnp.exp2(
+            coded[TILE - 1 : TILE] - CODE_TOP
         )
     squares = proj * proj
     largest = jnp.max(jnp.max(squares, axis=0, keepdims=True), axis=1, keepdims=True)
@@ -197,7 +239,7 @@
     )
     passed = passed & ((largest > 0.0) | (whole(fold(power)) <= 0.0))
     total = jnp.concatenate([proj, tail], axis=0)
-    norm_message(total, jnp.where(passed, 0.0, 1.0), *refs)
+    norm_message(total, jnp.where(passed, 0.0, 1.0), state_ref[0:1, :], *refs)
 
 
 def section_kernel(heard_ref, gain_ref, message_ref):
@@ -362,27 +404,26 @@
         for residue in range(GROUP)
     ]
 
-    proj = proj_grads[0, 0].reshape(micro, chips // GROUP, 2 * GROUP, own, columns)
+    proj = proj_grads[0, 0].reshape(micro, chips // GROUP, GROUP, 2, own, columns)
     beta = beta_grads[0, 0]
     gain = gain_grads[0, 0, 0]
     rate, clip = learn_rate.reshape(1), clip_limit.reshape(1)
     states = (gain_master, gain_moment, gain_second)
     peers = tensor_size * sections
 
-    def chip_parts():
-        send, _ = pack(True, rate, clip, proj, beta, gain, rows + TILE)
-        kept, scalars = pack(False, rate, clip, proj, beta, gain, rows + TILE)
-        got = lax.ppermute(send, "shard", core_pairs)
-        return kept, got, scalars
-
-    def totals(kernel, value):
+    def chip_parts(proj, beta, gain, states):
+        send, tails, state = pack(proj, beta, gain, states, rows + TILE)
+        return held(tails), held(lax.ppermute(send, "shard", core_pairs)), held(state)
+
+    def totals(kernel, value, state):
         total, message = pl.pallas_call(
             kernel,
             out_shape=(near_f32((rows + TILE, LANES)), near_f32((peers, 1, LANES))),
-            in_specs=[VMEM] * 4,
+            in_specs=[VMEM, VMEM],
             out_specs=(VMEM, VMEM),
             name="norm",
-        )(held(value), *states)
+            compiler_params=SMALL,
+        )(held(value), state)
         heard = lax.all_to_all(message, ("tensor", "section"), 0, 0)
         gain_rows, squares = pl.pallas_call(
             section_kernel,
@@ -390,18 +431,20 @@
             in_specs=[VMEM],
             out_specs=(VMEM, VMEM),
             name="section",
+            compiler_params=SMALL,
         )(held(heard))
         return total, gain_rows, lax.all_to_all(squares, "shard", 0, 0)
 
-    def exact_totals(*_):
-        kept, got, _ = chip_parts()
+    def exact_totals(proj, beta, gain, states, _):
+        tails, got, state = chip_parts(proj, beta, gain, states)
         chip_sum = pl.pallas_call(
             add_kernel,
-            out_shape=near_f32(kept.shape),
-            in_specs=[VMEM, VMEM],
+            out_shape=f32((GROUP, GROUP, rows + TILE, LANES)),
+            in_specs=[VMEM] * 3,
             out_specs=VMEM,
             name="core_add",
-        )(kept, held(got))
+            compiler_params=SMALL,
+        )(proj, tails, got)
         by_near = lax.all_to_all(chip_sum, "shard", 0, 0, axis_index_groups=near)
         near_sum = pl.pallas_call(
             sum_kernel,
@@ -409,23 +452,31 @@
             in_specs=[VMEM],
             out_specs=VMEM,
             name="near",
+            compiler_params=SMALL,
         )(held(by_near))
         by_far = lax.all_to_all(near_sum, "shard", 0, 0, axis_index_groups=far)
-        return totals(exact_norm_kernel, by_far)
-
-    kept, got, scalars = chip_parts()
-    coded = pl.pallas_call(
+        return totals(exact_norm_kernel, by_far, state)
+
+    tails, got, state = chip_parts(proj, beta, gain, states)
+    coded, scalars = pl.pallas_call(
         code_kernel,
-        out_shape=near_f32((chips, rows + 2 * TILE, LANES)),
-        in_specs=[VMEM, VMEM],
-        out_specs=VMEM,
+        out_shape=(near_f32((chips, rows + TILE, LANES)), near_f32((TILE, LANES))),
+        in_specs=[SMEM, SMEM] + [VMEM] * 3,
+        out_specs=(VMEM, VMEM),
         name="code",
-    )(kept, held(got))
+        compiler_params=SMALL,
+    )(rate, clip, held(proj), tails, got)
     z_groups = [[2 * z + side for z in range(chips)] for side in range(2)]
     by_chip = lax.all_to_all(coded.astype(WIRE), "shard", 0, 0, axis_index_groups=z_groups)
-    quick = totals(coded_norm_kernel, by_chip.astype(jnp.float32))
-    failed = jnp.sum(quick[2][:, 0, LANES - 1]) > 0.0
-    total, gain_rows, squares = lax.cond(failed, exact_totals, lambda *given: given, *quick)
+    quick = totals(coded_norm_kernel, by_chip.astype(jnp.float32), state)
+    *again, norm = lax.optimization_barrier(
+        (proj, beta, gain, states, quick[2])
+    )
+    quick = (quick[0], quick[1], norm)
+    failed = jnp.sum(norm[:, 0, LANES - 1]) > 0.0
+    total, gain_rows, squares = lax.cond(
+        failed, exact_totals, lambda *given: given[-1], *again, quick
+    )
     counted = sections * (
         width * columns * tensor_size + heads_here * tensor_size * width + width
     )
@@ -442,17 +493,18 @@
         in_specs=[VMEM] * 10,
         out_specs=(VMEM,) * 11,
         name="update",
+        compiler_params=SMALL,
     )(
         held(scalars),
         held(squares),
         held(total),
         held(gain_rows),
-        held(proj_master[0]),
-        held(proj_moment[0]),
-        held(proj_second[0]),
-        held(beta_master[0]),
-        held(beta_moment[0]),
-        held(beta_second[0]),
+        proj_master[0],
+        proj_moment[0],
+        proj_second[0],
+        beta_master[0],
+        beta_moment[0],
+        beta_second[0],
     )
     sent = (outs[0].astype(jnp.float32) * WIRE_SCALE).astype(WIRE)
     gathered = lax.all_gather(sent, "shard", axis=0)
@@ -468,6 +520,7 @@
         in_specs=[VMEM],
         out_specs=(VMEM, VMEM),
         name="unpack",
+        compiler_params=SMALL,
     )(held(small))
     return (
         proj_weights.reshape(1, width, columns),

time: 133 us -> 126 us (0.947)
  blocking collectives: 87.4 us -> 105 us
  waiting for transfers between devices: 13.1 us -> 1.28 us
  starting transfers between devices: 15.9 us -> 8.79 us
  Pallas kernels: 8.36 us -> 5.44 us
  local copies, waits for them, and re-layouts: 2.51 us -> 0.88 us
    all_to_all x0 -> x1, blocking collectives: none -> 18.2 us  [totals(): return (total, gain_rows, lax.all_to_all(squares, 'shard', 0, 0))]
    all_to_all x1 -> x0, waiting for transfers between devices: 11.8 us -> none  [totals(): return (total, gain_rows, lax.all_to_all(squares, 'shard', 0, 0))]
    all_to_all x1 -> x0, starting transfers between devices: 7.13 us -> none  [totals(): return (total, gain_rows, lax.all_to_all(squares, 'shard', 0, 0))]
    pallas_call x3 -> x2, Pallas kernels: 5.85 us -> 3.55 us  [the longest x1 3.02 us: pack(): pl.pallas_call(pack_kernel, in_specs=[pl.BlockSpec(memory_space=pl.ANY)]...]
    unnamed x26 -> x24, local copies, waits for them, and re-layouts: 2.51 us -> 0.88 us
  transfers between devices with their start and end apart: 2 -> 1, of which waited for: 2 -> 1; matrix products, arithmetic and copies ran while one was open for 0% -> 0% of each run, Pallas kernels for 1% -> 0%
where the time goes in v5:
time: 126 us
  blocking collectives  105 us (83%)
  starting transfers between devices  8.79 us (7%)
  Pallas kernels  5.44 us (4%)
  between operations  2.77 us (2%)
  other arithmetic  2.12 us (2%)
  waiting for transfers between devices  1.28 us (1%)
    all_to_all x1, blocking collectives, per_device(): lax.all_to_all(coded.astype(WIRE), 'shard', 0, 0, axis_index_groups=z_gro...  42.3 us
    all_gather x1, blocking collectives, per_device(): gathered = lax.all_gather(sent, 'shard', axis=0)  31.3 us
    all_to_all x1, blocking collectives, totals(): return (total, gain_rows, lax.all_to_all(squares, 'shard', 0, 0))  18.2 us
    all_to_all x1, blocking collectives, totals(): heard = lax.all_to_all(message, ('tensor', 'section'), 0, 0)  13 us
    ppermute x1, starting transfers between devices, chip_parts(): lax.ppermute(send, 'shard', core_pairs)  8.79 us
    pallas_call x1, Pallas kernels, pack(): pl.pallas_call(pack_kernel, in_specs=[pl.BlockSpec(memory_space=pl.ANY)]...  3.02 us
  transfers between devices with their start and end apart: 1, of which 1 were waited for; matrix products, arithmetic and copies ran while one was open for 0% of the time, Pallas kernels for 0%

profile of v5, /device:TPU:1, one launch (start us, length us, event | category | flops | bytes accessed | tf_op | source)
XLA Modules:
  0.0 126.1 jit_solution(7548891187058745420)
XLA Ops:
  0.6 0.0 copy-start
  0.7 3.0 %pack.3 = (f32[16,136,128]{2,1,0:T(8,128)}, f32[8,2048]{1,0:T(8,128)S(1)}, f32[8,128]{1,0:T(8,128)S(1)}) custom-call(bf16[2,4,4,2,64,256]{5,4,3,2,1,0:T(8,128)(2,1)} %bitcast.24, bf16[2,4,2048]{2,1,0:T(4,128)(2,1)} %bitcast.36, bf16[2,2048]{1,0:T(2,128)(2,1)} %bitcast.38, f32[1,16]{1,0:T(1,128)} %gain_master_ref.1, f32[1,16]{1,0:T(1,128)} %gain_moment_ref.1, ...), custom_call_target="tpu_custom_call" | custom-call | tf_op jit(solution)/shard_map/pack/pallas_call | solution.py:119
  3.7 8.8 %collective-permute-start.1 = (f32[16,136,128]{2,1,0:T(8,128)}, f32[16,136,128]{2,1,0:T(8,128)S(1)}, u32[]{:S(2)}, u32[]{:S(2)}) collective-permute-start(f32[16,136,128]{2,1,0:T(8,128)} %get-tuple-element.77), channel_id=1, source_target_pairs={{0,16},{16,0},{32,48},{48,32},{64,80},{80,64},{96,112},{112,96},{1... | collective-permute-start | bytes 3342344 | tf_op jit(solution)/shard_map/ppermute | solution.py:416
  13.8 1.3 %collective-permute-done.1.got_ref = f32[16,136,128]{2,1,0:T(8,128)S(1)} collective-permute-done((f32[16,136,128]{2,1,0:T(8,128)}, f32[16,136,128]{2,1,0:T(8,128)S(1)}, u32[]{:S(2)}, u32[]{:S(2)}) %collective-permute-start.1) | collective-permute-done | bytes 1114144 | tf_op jit(solution)/shard_map/ppermute | solution.py:416
  15.0 0.0 copy-done
  15.1 0.5 code.1
  15.6 0.1 convert_element_type.27
  15.7 42.3 %all_to_all.35 = f16[16,136,128]{2,1,0:T(8,128)(2,1)S(1)} all-to-all(f16[16,136,128]{2,1,0:T(8,128)(2,1)S(1)} %convert_element_type.27), channel_id=1, replica_groups={{0,32,64,96,128,160,192,224,256,288,320,352,384,416,448,480},{16,48,80,..., dimensions={0} | all-to-all | bytes 1114112 | tf_op jit(solution)/shard_map/all_to_all | solution.py:470
  58.0 0.0 copy-start.7
  58.0 0.0 copy-start.8
  58.0 0.0 copy-start.9
  58.0 0.0 copy-start.10
  58.0 0.0 copy-start.11
  58.0 0.1 convert_element_type.28.in_ref
  58.1 0.3 norm.3
  58.5 13.0 %all_to_all.36.heard_ref = f32[16,1,128]{2,1,0:T(1,128)S(1)} all-to-all(f32[16,1,128]{2,1,0:T(1,128)S(1)} %get-tuple-element.81), channel_id=1, replica_groups=mesh['shard'=32,'tensor'=4,'section'=4] {'tensor','section'}, dimensions={0} | all-to-all | bytes 16384 | tf_op jit(solution)/shard_map/all_to_all | solution.py:427
  71.4 0.1 section.3
  71.5 18.2 %all_to_all.37 = f32[32,1,128]{2,1,0:T(1,128)S(1)} all-to-all(f32[32,1,128]{2,1,0:T(1,128)S(1)} %get-tuple-element.82), channel_id=1, replica_groups=mesh['shard'=32,'tensor'=4,'section'=4] {'shard'}, dimensions={0} | all-to-all | bytes 32768 | tf_op jit(solution)/shard_map/all_to_all | solution.py:436
  89.7 0.7 slice_reduce_fusion
  91.1 0.0 copy-done.7
  91.1 0.0 copy-done.8
  91.1 0.0 copy-done.9
  91.1 0.0 copy-done.10
  91.1 0.0 copy-done.11
  91.2 0.0 copy-start.1
  91.2 0.0 copy-start.2
  91.2 0.0 copy-start.3
  91.2 0.0 copy-start.4
  91.2 0.0 copy-start.5
  91.2 0.0 copy-start.6
  91.2 0.8 copy-done.1
  92.0 0.0 copy-done.2
  92.0 0.0 copy-done.3
  92.1 0.0 copy-done.4
  92.1 0.0 copy-done.5
  92.1 0.0 copy-done.6
  92.1 0.8 update.1
  92.9 31.3 %all-gather.2 = f16[2304,256]{1,0:T(8,128)(2,1)S(1)} all-gather(f16[72,256]{1,0:T(8,128)(2,1)S(1)} %multiply_convert_fusion.2), channel_id=2, replica_groups=mesh['shard'=32,'tensor'=4,'section'=4] {'shard'}, dimensions={0}, use_global_device_ids=true | all-gather | bytes 1216512 | tf_op jit(solution)/shard_map/all_gather | solution.py:510
  124.2 1.2 multiply_convert_fusion
  125.5 0.6 unpack.1
  (3 shorter events, 0.0 us)
Async XLA Ops:
  0.6 14.4 %copy-start = (bf16[1,1,2,2048,256]{4,3,2,1,0:T(8,128)(2,1)S(1)}, bf16[1,1,2,2048,256]{4,3,2,1,0:T(8,128)(2,1)}, u32[]{:S(2)}) copy-start(bf16[1,1,2,2048,256]{4,3,2,1,0:T(8,128)(2,1)} %param.16) | copy-start | bytes 6291460
  3.7 11.4 %collective-permute-start.1 = (f32[16,136,128]{2,1,0:T(8,128)}, f32[16,136,128]{2,1,0:T(8,128)S(1)}, u32[]{:S(2)}, u32[]{:S(2)}) collective-permute-start(f32[16,136,128]{2,1,0:T(8,128)} %get-tuple-element.77), channel_id=1, source_target_pairs={{0,16},{16,0},{32,48},{48,32},{64,80},{80,64},{96,112},{112,96},{1... | collective-permute-start | bytes 3342344 | tf_op jit(solution)/shard_map/ppermute | solution.py:416
  58.0 33.1 %copy-start.7 = (bf16[1,1,2,4,2048]{4,3,2,1,0:T(4,128)(2,1)S(1)}, bf16[1,1,2,4,2048]{4,3,2,1,0:T(4,128)(2,1)}, u32[]{:S(2)}) copy-start(bf16[1,1,2,4,2048]{4,3,2,1,0:T(4,128)(2,1)} %param.17) | copy-start | bytes 98308
  58.0 33.1 %copy-start.8 = (bf16[1,1,1,2,2048]{4,3,2,1,0:T(2,128)(2,1)S(1)}, bf16[1,1,1,2,2048]{4,3,2,1,0:T(2,128)(2,1)}, u32[]{:S(2)}) copy-start(bf16[1,1,1,2,2048]{4,3,2,1,0:T(2,128)(2,1)} %param.18) | copy-start | bytes 24580
  58.0 33.1 %copy-start.9 = (f32[1,16]{1,0:T(1,128)S(1)}, f32[1,16]{1,0:T(1,128)}, u32[]{:S(2)}) copy-start(f32[1,16]{1,0:T(1,128)} %gain_master_ref.1) | copy-start | bytes 196
  58.0 33.1 %copy-start.10 = (f32[1,16]{1,0:T(1,128)S(1)}, f32[1,16]{1,0:T(1,128)}, u32[]{:S(2)}) copy-start(f32[1,16]{1,0:T(1,128)} %gain_moment_ref.1) | copy-start | bytes 196
  58.0 33.1 %copy-start.11 = (f32[1,16]{1,0:T(1,128)S(1)}, f32[1,16]{1,0:T(1,128)}, u32[]{:S(2)}) copy-start(f32[1,16]{1,0:T(1,128)} %gain_second_ref.1) | copy-start | bytes 196
  91.2 0.8 copy-start.1
  91.2 0.9 copy-start.2
  91.2 0.9 copy-start.3
  91.2 0.9 copy-start.4
  91.2 0.9 copy-start.5
  91.2 0.9 copy-start.6

commit v6 on v5

--- a/solution.py
+++ b/solution.py
@@ -58,13 +58,6 @@
 def stack_halves(rows):
     return jnp.concatenate(
         [rows[:, start : start + LANES] for start in range(0, rows.shape[1], LANES)], axis=0
-    )
-
-
-def proj_rows(proj_ref, chip, core):
-    place = (chip // GROUP, chip % GROUP, core)
-    return stack_halves(
-        proj_ref[(0,) + place].astype(jnp.float32) + proj_ref[(1,) + place].astype(jnp.float32)
     )
 
 
@@ -76,55 +69,45 @@
     gain_moment_ref,
     gain_second_ref,
     out_ref,
-    tails_ref,
     state_ref,
     buffer,
-    staged,
     arrived,
-    sent,
+    *,
+    flip,
 ):
-    other = 1 - lax.axis_index("shard") % 2
+    core = lax.axis_index("shard") % 2
+    which = 1 - core if flip else core
     arrivals = [
         pltpu.make_async_copy(
-            proj_ref.at[:, high, :, other], buffer.at[high], arrived.at[high]
+            proj_ref.at[:, high, :, which], buffer.at[high], arrived.at[high]
         )
         for high in range(GROUP)
     ]
     for copy in arrivals:
         copy.start()
     tails = tail_rows(beta_ref, gain_ref)
-    tails_ref[...] = tails
     state = gain_state_row(gain_master_ref, gain_moment_ref, gain_second_ref)
     state_ref[...] = jnp.broadcast_to(state, state_ref.shape)
-    rows = staged.shape[1] - TILE
-    departures = []
+    rows = out_ref.shape[1] - TILE
     for high in range(GROUP):
         arrivals[high].wait()
         for low in range(GROUP):
             chip = high * GROUP + low
-            staged[chip, :rows, :] = stack_halves(
+            out_ref[chip, :rows, :] = stack_halves(
                 buffer[high, 0, low].astype(jnp.float32) + buffer[high, 1, low].astype(jnp.float32)
             )
-            staged[chip, rows:, :] = tails[:, chip * LANES : (chip + 1) * LANES]
-        part = pl.ds(high * GROUP, GROUP)
-        departures.append(pltpu.make_async_copy(staged.at[part], out_ref.at[part], sent.at[high]))
-        departures[-1].start()
-    for copy in departures:
-        copy.wait()
-
-
-def pack(proj, beta, gain, states, rows):
+            out_ref[chip, rows:, :] = tails[:, chip * LANES : (chip + 1) * LANES]
+
+
+def pack(flip, proj, beta, gain, states, rows):
     own, columns = proj.shape[4:]
-    shape = (GROUP * GROUP, rows, LANES)
     return pl.pallas_call(
-        pack_kernel,
+        functools.partial(pack_kernel, flip=flip),
         in_specs=[pl.BlockSpec(memory_space=pl.ANY)] + [VMEM] * 5,
-        out_specs=(pl.BlockSpec(memory_space=pl.ANY), VMEM, VMEM),
-        out_shape=(f32(shape), near_f32((TILE, gain.shape[1])), near_f32((TILE, LANES))),
+        out_specs=(VMEM, VMEM),
+        out_shape=(near_f32((GROUP * GROUP, rows, LANES)), near_f32((TILE, LANES))),
         scratch_shapes=[
             pltpu.VMEM((GROUP, 2, GROUP, own, columns), jnp.bfloat16),
-            pltpu.VMEM(shape, jnp.float32),
-            pltpu.SemaphoreType.DMA((GROUP,)),
             pltpu.SemaphoreType.DMA((GROUP,)),
         ],
         name="pack",
@@ -143,7 +126,7 @@
     return jnp.concatenate([jnp.zeros((1, LANES - 3 * share), jnp.float32)] + states, axis=1)
 
 
-def code_kernel(rate_ref, clip_ref, proj_ref, tails_ref, got_ref, out_ref, scalars_ref):
+def code_kernel(rate_ref, clip_ref, kept_ref, got_ref, out_ref, scalars_ref):
     row = lax.broadcasted_iota(jnp.int32, (TILE, LANES), 0)
     scalars_ref[...] = jnp.where(row == 0, rate_ref[0], clip_ref[0])
     rows = got_ref.shape[1] - TILE
@@ -151,8 +134,8 @@
     core = lax.axis_index("shard") % 2
     left_half = lax.broadcasted_iota(jnp.int32, (TILE, LANES), 1) < own
     for chip in range(GROUP * GROUP):
-        proj = proj_rows(proj_ref, chip, core) + got_ref[chip, :rows, :]
-        tail = tails_ref[:, chip * LANES : (chip + 1) * LANES] + got_ref[chip, rows:, :]
+        proj = kept_ref[chip, :rows, :] + got_ref[chip, :rows, :]
+        tail = kept_ref[chip, rows:, :] + got_ref[chip, rows:, :]
         tail = pltpu.roll(tail, LANES - core * own, 1)
         proj_scale, tail_scale = block_scale(proj), block_scale(tail)
         out_ref[chip, :rows, :] = proj * jnp.exp2(CODE_TOP - proj_scale)
@@ -164,14 +147,9 @@
         out_ref[chip, rows:, :] = tail
 
 
-def add_kernel(proj_ref, tails_ref, got_ref, out_ref):
-    rows = got_ref.shape[1] - TILE
-    core = lax.axis_index("shard") % 2
+def add_kernel(kept_ref, got_ref, out_ref):
     for chip in range(GROUP * GROUP):
-        place = (chip % GROUP, chip // GROUP)
-        tail = tails_ref[:, chip * LANES : (chip + 1) * LANES]
-        out_ref[place + (slice(0, rows),)] = proj_rows(proj_ref, chip, core) + got_ref[chip, :rows, :]
-        out_ref[place + (slice(rows, None),)] = tail + got_ref[chip, rows:, :]
+        out_ref[chip % GROUP, chip // GROUP] = kept_ref[chip] + got_ref[chip]
 
 
 def sum_kernel(in_ref, out_ref):
@@ -412,8 +390,9 @@
     peers = tensor_size * sections
 
     def chip_parts(proj, beta, gain, states):
-        send, tails, state = pack(proj, beta, gain, states, rows + TILE)
-        return held(tails), held(lax.ppermute(send, "shard", core_pairs)), held(state)
+        send, state = pack(True, proj, beta, gain, states, rows + TILE)
+        kept, _ = pack(False, proj, beta, gain, states, rows + TILE)
+        return held(kept), held(lax.ppermute(send, "shard", core_pairs)), held(state)
 
     def totals(kernel, value, state):
         total, message = pl.pallas_call(
@@ -436,15 +415,15 @@
         return total, gain_rows, lax.all_to_all(squares, "shard", 0, 0)
 
     def exact_totals(proj, beta, gain, states, _):
-        tails, got, state = chip_parts(proj, beta, gain, states)
+        kept, got, state = chip_parts(proj, beta, gain, states)
         chip_sum = pl.pallas_call(
             add_kernel,
             out_shape=f32((GROUP, GROUP, rows + TILE, LANES)),
-            in_specs=[VMEM] * 3,
+            in_specs=[VMEM] * 2,
             out_specs=VMEM,
             name="core_add",
             compiler_params=SMALL,
-        )(proj, tails, got)
+        )(kept, got)
         by_near = lax.all_to_all(chip_sum, "shard", 0, 0, axis_index_groups=near)
         near_sum = pl.pallas_call(
             sum_kernel,
@@ -457,15 +436,15 @@
         by_far = lax.all_to_all(near_sum, "shard", 0, 0, axis_index_groups=far)
         return totals(exact_norm_kernel, by_far, state)
 
-    tails, got, state = chip_parts(proj, beta, gain, states)
+    kept, got, state = chip_parts(proj, beta, gain, states)
     coded, scalars = pl.pallas_call(
         code_kernel,
         out_shape=(near_f32((chips, rows + TILE, LANES)), near_f32((TILE, LANES))),
-        in_specs=[SMEM, SMEM] + [VMEM] * 3,
+        in_specs=[SMEM, SMEM, VMEM, VMEM],
         out_specs=(VMEM, VMEM),
         name="code",
         compiler_params=SMALL,
-    )(rate, clip, held(proj), tails, got)
+    )(rate, clip, kept, got)
     z_groups = [[2 * z + side for z in range(chips)] for side in range(2)]
     by_chip = lax.all_to_all(coded.astype(WIRE), "shard", 0, 0, axis_index_groups=z_groups)
     quick = totals(coded_norm_kernel, by_chip.astype(jnp.float32), state)

time: 126 us -> 125 us (level)
    pallas_call x1 -> x2, Pallas kernels: 3.02 us -> 3.06 us  [pack(): pl.pallas_call(functools.partial(pack_kernel, flip=flip), in_specs=[pl.Bl...]
  transfers between devices with their start and end apart: 1 -> 1, of which waited for: 1 -> 1; matrix products, arithmetic and copies ran while one was open for 0% -> 0% of each run, Pallas kernels for 0% -> 1%
where the time goes in v6:
time: 125 us
  blocking collectives  105 us (84%)
  starting transfers between devices  8.79 us (7%)
  Pallas kernels  5.49 us (4%)
  between operations  2.81 us (2%)
  other arithmetic  2.12 us (2%)
    all_to_all x1, blocking collectives, per_device(): lax.all_to_all(coded.astype(WIRE), 'shard', 0, 0, axis_index_groups=z_gro...  42.3 us
    all_gather x1, blocking collectives, per_device(): gathered = lax.all_gather(sent, 'shard', axis=0)  31.3 us
    all_to_all x1, blocking collectives, totals(): return (total, gain_rows, lax.all_to_all(squares, 'shard', 0, 0))  18.2 us
    all_to_all x1, blocking collectives, totals(): heard = lax.all_to_all(message, ('tensor', 'section'), 0, 0)  13 us
    ppermute x1, starting transfers between devices, chip_parts(): lax.ppermute(send, 'shard', core_pairs)  8.79 us
    pallas_call x2, Pallas kernels, pack(): pl.pallas_call(functools.partial(pack_kernel, flip=flip), in_specs=[pl.Bl...  3.06 us
  transfers between devices with their start and end apart: 1, of which 1 were waited for; matrix products, arithmetic and copies ran while one was open for 0% of the time, Pallas kernels for 1%

profile of v6, /device:TPU:1, one launch (start us, length us, event | category | flops | bytes accessed | tf_op | source)
XLA Modules:
  0.0 125.0 jit_solution(2204022731814198650)
XLA Ops:
  0.6 0.0 copy-start.6
  0.7 0.0 copy-start.7
  0.7 0.0 copy-start.8
  0.7 0.0 copy-start.9
  0.7 0.0 copy-start.10
  0.7 0.0 copy-start.11
  0.7 2.2 %pack.7 = (f32[16,136,128]{2,1,0:T(8,128)S(1)}, f32[8,128]{1,0:T(8,128)S(1)}) custom-call(bf16[2,4,4,2,64,256]{5,4,3,2,1,0:T(8,128)(2,1)} %bitcast.30, bf16[2,4,2048]{2,1,0:T(4,128)(2,1)} %bitcast.36, bf16[2,2048]{1,0:T(2,128)(2,1)} %bitcast.39, f32[1,16]{1,0:T(1,128)} %gain_master_ref.3, f32[1,16]{1,0:T(1,128)} %gain_moment_ref.3, f32[1,16]{1,0:T(1,128)} %gain_second_ref.3), custom_call_target="tpu_custom_call" | custom-call | tf_op jit(solution)/shard_map/pack/pallas_call | solution.py:104
  2.9 8.8 %collective-permute-start.1 = (f32[16,136,128]{2,1,0:T(8,128)S(1)}, f32[16,136,128]{2,1,0:T(8,128)S(1)}, u32[]{:S(2)}, u32[]{:S(2)}) collective-permute-start(f32[16,136,128]{2,1,0:T(8,128)S(1)} %get-tuple-element.77), channel_id=1, source_target_pairs={{0,16},{16,0},{32,48},{48,32},{64,80},{80,64},{96,112},{112,96},{1... | collective-permute-start | bytes 3342344 | tf_op jit(solution)/shard_map/ppermute | solution.py:395
  11.7 0.0 copy-done.6
  11.7 0.0 copy-done.7
  11.7 0.0 copy-done.8
  11.7 0.0 copy-done.9
  11.7 0.0 copy-done.10
  11.7 0.0 copy-done.11
  11.8 0.9 pack.6
  13.9 0.1 collective-permute-done.1.got_ref
  14.1 0.5 code.1
  14.6 0.1 convert_element_type.27
  14.7 42.3 %all_to_all.35 = f16[16,136,128]{2,1,0:T(8,128)(2,1)S(1)} all-to-all(f16[16,136,128]{2,1,0:T(8,128)(2,1)S(1)} %convert_element_type.27), channel_id=1, replica_groups={{0,32,64,96,128,160,192,224,256,288,320,352,384,416,448,480},{16,48,80,..., dimensions={0} | all-to-all | bytes 1114112 | tf_op jit(solution)/shard_map/all_to_all | solution.py:449
  57.0 0.1 convert_element_type.28.in_ref
  57.1 0.3 norm.3
  57.4 13.0 %all_to_all.36.heard_ref = f32[16,1,128]{2,1,0:T(1,128)S(1)} all-to-all(f32[16,1,128]{2,1,0:T(1,128)S(1)} %get-tuple-element.81), channel_id=1, replica_groups=mesh['shard'=32,'tensor'=4,'section'=4] {'tensor','section'}, dimensions={0} | all-to-all | bytes 16384 | tf_op jit(solution)/shard_map/all_to_all | solution.py:406
  70.4 0.1 section.3
  70.5 18.2 %all_to_all.37 = f32[32,1,128]{2,1,0:T(1,128)S(1)} all-to-all(f32[32,1,128]{2,1,0:T(1,128)S(1)} %get-tuple-element.82), channel_id=1, replica_groups=mesh['shard'=32,'tensor'=4,'section'=4] {'shard'}, dimensions={0} | all-to-all | bytes 32768 | tf_op jit(solution)/shard_map/all_to_all | solution.py:415
  88.7 0.7 slice_reduce_fusion
  90.1 0.0 copy-start
  90.1 0.0 copy-start.1
  90.1 0.0 copy-start.2
  90.1 0.0 copy-start.3
  90.1 0.0 copy-start.4
  90.1 0.0 copy-start.5
  90.2 0.8 copy-done
  90.9 0.0 copy-done.1
  91.0 0.0 copy-done.2
  91.0 0.0 copy-done.3
  91.0 0.0 copy-done.4
  91.0 0.0 copy-done.5
  91.0 0.8 update.1
  91.9 31.3 %all-gather.2 = f16[2304,256]{1,0:T(8,128)(2,1)S(1)} all-gather(f16[72,256]{1,0:T(8,128)(2,1)S(1)} %multiply_convert_fusion.2), channel_id=2, replica_groups=mesh['shard'=32,'tensor'=4,'section'=4] {'shard'}, dimensions={0}, use_global_device_ids=true | all-gather | bytes 1216512 | tf_op jit(solution)/shard_map/all_gather | solution.py:489
  123.1 1.2 multiply_convert_fusion
  124.4 0.6 unpack.1
  (3 shorter events, 0.0 us)
Async XLA Ops:
  0.6 11.1 %copy-start.6 = (bf16[1,1,2,2048,256]{4,3,2,1,0:T(8,128)(2,1)S(1)}, bf16[1,1,2,2048,256]{4,3,2,1,0:T(8,128)(2,1)}, u32[]{:S(2)}) copy-start(bf16[1,1,2,2048,256]{4,3,2,1,0:T(8,128)(2,1)} %param.16) | copy-start | bytes 6291460
  0.7 11.0 %copy-start.7 = (bf16[1,1,2,4,2048]{4,3,2,1,0:T(4,128)(2,1)S(1)}, bf16[1,1,2,4,2048]{4,3,2,1,0:T(4,128)(2,1)}, u32[]{:S(2)}) copy-start(bf16[1,1,2,4,2048]{4,3,2,1,0:T(4,128)(2,1)} %param.17) | copy-start | bytes 98308
  0.7 11.0 %copy-start.8 = (bf16[1,1,1,2,2048]{4,3,2,1,0:T(2,128)(2,1)S(1)}, bf16[1,1,1,2,2048]{4,3,2,1,0:T(2,128)(2,1)}, u32[]{:S(2)}) copy-start(bf16[1,1,1,2,2048]{4,3,2,1,0:T(2,128)(2,1)} %param.18) | copy-start | bytes 24580
  0.7 11.0 %copy-start.9 = (f32[1,16]{1,0:T(1,128)S(1)}, f32[1,16]{1,0:T(1,128)}, u32[]{:S(2)}) copy-start(f32[1,16]{1,0:T(1,128)} %gain_master_ref.3) | copy-start | bytes 196
  0.7 11.0 %copy-start.10 = (f32[1,16]{1,0:T(1,128)S(1)}, f32[1,16]{1,0:T(1,128)}, u32[]{:S(2)}) copy-start(f32[1,16]{1,0:T(1,128)} %gain_moment_ref.3) | copy-start | bytes 196
  0.7 11.0 %copy-start.11 = (f32[1,16]{1,0:T(1,128)S(1)}, f32[1,16]{1,0:T(1,128)}, u32[]{:S(2)}) copy-start(f32[1,16]{1,0:T(1,128)} %gain_second_ref.3) | copy-start | bytes 196
  2.9 11.2 %collective-permute-start.1 = (f32[16,136,128]{2,1,0:T(8,128)S(1)}, f32[16,136,128]{2,1,0:T(8,128)S(1)}, u32[]{:S(2)}, u32[]{:S(2)}) collective-permute-start(f32[16,136,128]{2,1,0:T(8,128)S(1)} %get-tuple-element.77), channel_id=1, source_target_pairs={{0,16},{16,0},{32,48},{48,32},{64,80},{80,64},{96,112},{112,96},{1... | collective-permute-start | bytes 3342344 | tf_op jit(solution)/shard_map/ppermute | solution.py:395
  90.1 0.8 copy-start
  90.1 0.9 copy-start.1
  90.1 0.9 copy-start.2
  90.1 0.9 copy-start.3
  90.1 0.9 copy-start.4
  90.1 0.9 copy-start.5

commit v7 on v6

--- a/solution.py
+++ b/solution.py
@@ -253,6 +253,17 @@
     total = jnp.where(lane == LANES - 1, failed, total)
     for peer in range(message_ref.shape[0]):
         message_ref[peer] = total
+
+
+def flag_kernel(squares_ref, *refs):
+    half = len(refs) // 2
+    flag_ref = refs[half]
+    for state_ref, held_ref in zip(refs[:half], refs[half + 1 :]):
+        held_ref[...] = state_ref[...]
+    rows = jnp.sum(squares_ref[...], axis=0)
+    lane = lax.broadcasted_iota(jnp.int32, rows.shape, 1)
+    failed = jnp.max(jnp.where(lane == LANES - 1, rows, 0.0))
+    flag_ref[0] = jnp.where(failed > 0.0, 1, 0)
 
 
 def update_kernel(
@@ -452,7 +463,27 @@
         (proj, beta, gain, states, quick[2])
     )
     quick = (quick[0], quick[1], norm)
-    failed = jnp.sum(norm[:, 0, LANES - 1]) > 0.0
+    own_states = [
+        value[0]
+        for value in (
+            proj_master,
+            proj_moment,
+            proj_second,
+            beta_master,
+            beta_moment,
+            beta_second,
+        )
+    ]
+    flag, *own_states = pl.pallas_call(
+        flag_kernel,
+        out_shape=(jax.ShapeDtypeStruct((1,), jnp.int32),)
+        + tuple(near_f32(value.shape) for value in own_states),
+        in_specs=[VMEM] * 7,
+        out_specs=(SMEM,) + (VMEM,) * 6,
+        name="flag",
+        compiler_params=SMALL,
+    )(held(norm), *own_states)
+    failed = flag[0] > 0
     total, gain_rows, squares = lax.cond(
         failed, exact_totals, lambda *given: given[-1], *again, quick
     )
@@ -478,12 +509,7 @@
         held(squares),
         held(total),
         held(gain_rows),
-        proj_master[0],
-        proj_moment[0],
-        proj_second[0],
-        beta_master[0],
-        beta_moment[0],
-        beta_second[0],
+        *[held(value) for value in own_states],
     )
     sent = (outs[0].astype(jnp.float32) * WIRE_SCALE).astype(WIRE)
     gathered = lax.all_gather(sent, "shard", axis=0)

time: 125 us -> 125 us (level)
  no operation moved by 1% of the time
where the time goes in v7:
time: 125 us; the launch traced here: 124 us
  blocking collectives  105 us (84%)
  starting transfers between devices  8.79 us (7%)
  Pallas kernels  6.18 us (5%)
  between operations  2.82 us (2%)
  other arithmetic  1.42 us (1%)
    all_to_all x1, blocking collectives, per_device(): lax.all_to_all(coded.astype(WIRE), 'shard', 0, 0, axis_index_groups=z_gro...  42.3 us
    all_gather x1, blocking collectives, per_device(): gathered = lax.all_gather(sent, 'shard', axis=0)  31.3 us
    all_to_all x1, blocking collectives, totals(): return (total, gain_rows, lax.all_to_all(squares, 'shard', 0, 0))  18.2 us
    all_to_all x1, blocking collectives, totals(): heard = lax.all_to_all(message, ('tensor', 'section'), 0, 0)  13 us
    ppermute x1, starting transfers between devices, chip_parts(): lax.ppermute(send, 'shard', core_pairs)  8.79 us
    pallas_call x2, Pallas kernels, pack(): pl.pallas_call(functools.partial(pack_kernel, flip=flip), in_specs=[pl.Bl...  3.06 us
  transfers between devices with their start and end apart: 1, of which 1 were waited for; matrix products, arithmetic and copies ran while one was open for 0% of the time, Pallas kernels for 1%

profile of v7, /device:TPU:1, one launch (start us, length us, event | category | flops | bytes accessed | tf_op | source)
XLA Modules:
  0.0 124.2 jit_solution(5452481480575789438)
XLA Ops:
  0.6 0.0 copy-start.6
  0.7 0.0 copy-start.8
  0.7 0.0 copy-start.9
  0.7 0.0 copy-start.10
  0.7 0.0 copy-start.11
  0.7 0.0 copy-start.12
  0.7 2.2 %pack.7 = (f32[16,136,128]{2,1,0:T(8,128)S(1)}, f32[8,128]{1,0:T(8,128)S(1)}) custom-call(bf16[2,4,4,2,64,256]{5,4,3,2,1,0:T(8,128)(2,1)} %bitcast.31, bf16[2,4,2048]{2,1,0:T(4,128)(2,1)} %bitcast.37, bf16[2,2048]{1,0:T(2,128)(2,1)} %bitcast.40, f32[1,16]{1,0:T(1,128)} %gain_master_ref.3, f32[1,16]{1,0:T(1,128)} %gain_moment_ref.3, f32[1,16]{1,0:T(1,128)} %gain_second_ref.3), custom_call_target="tpu_custom_call" | custom-call | tf_op jit(solution)/shard_map/pack/pallas_call | solution.py:104
  2.9 8.8 %collective-permute-start.1 = (f32[16,136,128]{2,1,0:T(8,128)S(1)}, f32[16,136,128]{2,1,0:T(8,128)S(1)}, u32[]{:S(2)}, u32[]{:S(2)}) collective-permute-start(f32[16,136,128]{2,1,0:T(8,128)S(1)} %get-tuple-element.84), channel_id=1, source_target_pairs={{0,16},{16,0},{32,48},{48,32},{64,80},{80,64},{96,112},{112,96},{1... | collective-permute-start | bytes 3342344 | tf_op jit(solution)/shard_map/ppermute | solution.py:406
  11.7 0.0 copy-done.6
  11.7 0.0 copy-done.8
  11.7 0.0 copy-done.9
  11.7 0.0 copy-done.10
  11.7 0.0 copy-done.11
  11.7 0.0 copy-done.12
  11.8 0.9 pack.6
  13.9 0.1 collective-permute-done.1.got_ref
  14.1 0.5 code.1
  14.6 0.1 convert_element_type.30
  14.7 42.3 %all_to_all.35 = f16[16,136,128]{2,1,0:T(8,128)(2,1)S(1)} all-to-all(f16[16,136,128]{2,1,0:T(8,128)(2,1)S(1)} %convert_element_type.30), channel_id=1, replica_groups={{0,32,64,96,128,160,192,224,256,288,320,352,384,416,448,480},{16,48,80,..., dimensions={0} | all-to-all | bytes 1114112 | tf_op jit(solution)/shard_map/all_to_all | solution.py:460
  57.0 0.0 copy-start
  57.0 0.0 copy-start.1
  57.0 0.0 copy-start.2
  57.0 0.0 copy-start.3
  57.0 0.0 copy-start.4
  57.0 0.0 copy-start.5
  57.1 0.1 convert_element_type.31.in_ref
  57.1 0.3 norm.3
  57.5 13.0 %all_to_all.36.heard_ref = f32[16,1,128]{2,1,0:T(1,128)S(1)} all-to-all(f32[16,1,128]{2,1,0:T(1,128)S(1)} %get-tuple-element.88), channel_id=1, replica_groups=mesh['shard'=32,'tensor'=4,'section'=4] {'tensor','section'}, dimensions={0} | all-to-all | bytes 16384 | tf_op jit(solution)/shard_map/all_to_all | solution.py:417
  70.4 0.1 section.3
  70.5 18.2 %all_to_all.37.squares_ref = f32[32,1,128]{2,1,0:T(1,128)S(1)} all-to-all(f32[32,1,128]{2,1,0:T(1,128)S(1)} %get-tuple-element.89), channel_id=1, replica_groups=mesh['shard'=32,'tensor'=4,'section'=4] {'shard'}, dimensions={0} | all-to-all | bytes 32768 | tf_op jit(solution)/shard_map/all_to_all | solution.py:426
  88.8 0.0 copy-done
  88.8 0.0 copy-done.1
  88.8 0.0 copy-done.2
  88.8 0.0 copy-done.3
  88.8 0.0 copy-done.4
  88.8 0.0 copy-done.5
  88.8 0.7 flag.1
  90.2 0.8 update.1
  91.0 31.3 %all-gather.2 = f16[2304,256]{1,0:T(8,128)(2,1)S(1)} all-gather(f16[72,256]{1,0:T(8,128)(2,1)S(1)} %multiply_convert_fusion.2), channel_id=2, replica_groups=mesh['shard'=32,'tensor'=4,'section'=4] {'shard'}, dimensions={0}, use_global_device_ids=true | all-gather | bytes 1216512 | tf_op jit(solution)/shard_map/all_gather | solution.py:515
  122.3 1.2 multiply_convert_fusion
  123.6 0.6 unpack.1
  (3 shorter events, 0.0 us)
Async XLA Ops:
  0.6 11.1 %copy-start.6 = (bf16[1,1,2,2048,256]{4,3,2,1,0:T(8,128)(2,1)S(1)}, bf16[1,1,2,2048,256]{4,3,2,1,0:T(8,128)(2,1)}, u32[]{:S(2)}) copy-start(bf16[1,1,2,2048,256]{4,3,2,1,0:T(8,128)(2,1)} %param.16) | copy-start | bytes 6291460
  0.7 11.0 %copy-start.8 = (bf16[1,1,2,4,2048]{4,3,2,1,0:T(4,128)(2,1)S(1)}, bf16[1,1,2,4,2048]{4,3,2,1,0:T(4,128)(2,1)}, u32[]{:S(2)}) copy-start(bf16[1,1,2,4,2048]{4,3,2,1,0:T(4,128)(2,1)} %param.17) | copy-start | bytes 98308
  0.7 11.0 %copy-start.9 = (bf16[1,1,1,2,2048]{4,3,2,1,0:T(2,128)(2,1)S(1)}, bf16[1,1,1,2,2048]{4,3,2,1,0:T(2,128)(2,1)}, u32[]{:S(2)}) copy-start(bf16[1,1,1,2,2048]{4,3,2,1,0:T(2,128)(2,1)} %param.18) | copy-start | bytes 24580
  0.7 11.0 %copy-start.10 = (f32[1,16]{1,0:T(1,128)S(1)}, f32[1,16]{1,0:T(1,128)}, u32[]{:S(2)}) copy-start(f32[1,16]{1,0:T(1,128)} %gain_master_ref.3) | copy-start | bytes 196
  0.7 11.0 %copy-start.11 = (f32[1,16]{1,0:T(1,128)S(1)}, f32[1,16]{1,0:T(1,128)}, u32[]{:S(2)}) copy-start(f32[1,16]{1,0:T(1,128)} %gain_moment_ref.3) | copy-start | bytes 196
  0.7 11.0 %copy-start.12 = (f32[1,16]{1,0:T(1,128)S(1)}, f32[1,16]{1,0:T(1,128)}, u32[]{:S(2)}) copy-start(f32[1,16]{1,0:T(1,128)} %gain_second_ref.3) | copy-start | bytes 196
  2.9 11.2 %collective-permute-start.1 = (f32[16,136,128]{2,1,0:T(8,128)S(1)}, f32[16,136,128]{2,1,0:T(8,128)S(1)}, u32[]{:S(2)}, u32[]{:S(2)}) collective-permute-start(f32[16,136,128]{2,1,0:T(8,128)S(1)} %get-tuple-element.84), channel_id=1, source_target_pairs={{0,16},{16,0},{32,48},{48,32},{64,80},{80,64},{96,112},{112,96},{1... | collective-permute-start | bytes 3342344 | tf_op jit(solution)/shard_map/ppermute | solution.py:406
  57.0 31.7 %copy-start = (f32[1,64,256]{2,1,0:T(8,128)S(1)}, f32[1,64,256]{2,1,0:T(8,128)}, u32[]{:S(2)}) copy-start(f32[1,64,256]{2,1,0:T(8,128)} %param.19) | copy-start | bytes 196612
  57.0 31.8 %copy-start.1 = (f32[1,64,256]{2,1,0:T(8,128)S(1)}, f32[1,64,256]{2,1,0:T(8,128)}, u32[]{:S(2)}) copy-start(f32[1,64,256]{2,1,0:T(8,128)} %param.20) | copy-start | bytes 196612
  57.0 31.8 %copy-start.2 = (f32[1,64,256]{2,1,0:T(8,128)S(1)}, f32[1,64,256]{2,1,0:T(8,128)}, u32[]{:S(2)}) copy-start(f32[1,64,256]{2,1,0:T(8,128)} %param.21) | copy-start | bytes 196612
  57.0 31.8 %copy-start.3 = (f32[1,4,64]{2,1,0:T(4,128)S(1)}, f32[1,4,64]{2,1,0:T(4,128)}, u32[]{:S(2)}) copy-start(f32[1,4,64]{2,1,0:T(4,128)} %param.22) | copy-start | bytes 3076
  57.0 31.8 %copy-start.4 = (f32[1,4,64]{2,1,0:T(4,128)S(1)}, f32[1,4,64]{2,1,0:T(4,128)}, u32[]{:S(2)}) copy-start(f32[1,4,64]{2,1,0:T(4,128)} %param.23) | copy-start | bytes 3076
  57.0 31.8 %copy-start.5 = (f32[1,4,64]{2,1,0:T(4,128)S(1)}, f32[1,4,64]{2,1,0:T(4,128)}, u32[]{:S(2)}) copy-start(f32[1,4,64]{2,1,0:T(4,128)} %param.24) | copy-start | bytes 3076
